TPU v7x, 128 devices: a whole 4x4x4 slice. The times are simulated.
128 devices in a mesh: oi: 8 (over x, z_lo), oj: 16 (over z_hi, y, core).
Axes of the slice: x: 4, y: 4, z: 4 (z_hi: 2, z_lo: 2; z = z_hi * 2 + z_lo), core: 2. Of those that a mesh axis runs over, the one named last changes fastest.
Arguments:
- amplitudes: bfloat16 [256, 256, 1024], P('oj', 'oi'), may hold values from -0.15625 to 0.15625
- exchange_ints: bfloat16 [256, 256, 1024], P('oj', 'oi'), may hold values from -6 to 6
- hole_factors: bfloat16 [1024, 1024], P(('oi', 'oj')), may hold values from -4 to 4
- occ_energy: float32 [32], replicated, may hold values from -2 to -0.5
- vir_energy: float32 [256], replicated, may hold values from 0.2 to 3
Outputs:
- amplitude_update: float32 [256, 256, 1024], P('oj', None, 'oi')
All inputs are finite; a program needn't handle non-finite values.
Results may differ from a plain program's by a relative error of at most 0.0039.
Values may be sent and summed in bfloat16 or wider, within the bound.
No kernel may reach another device: no remote copies, remote signals or barrier semaphores. Data moves between devices by JAX's collectives and lax.ppermute only.
A program may use at most 128 MiB of HBM per device.

v0:
```python
import jax
import jax.numpy as jnp
from jax import lax
from jax.sharding import PartitionSpec as P


def local(amplitudes, exchange_ints, hole_factors, occ_energy, vir_energy):
    virt_tile, virt_cols, pair_count = amplitudes.shape
    occupied = occ_energy.shape[0]
    virtual = vir_energy.shape[0]
    amp_matrix = amplitudes.reshape(virt_tile * virt_cols, pair_count)
    ints_matrix = exchange_ints.reshape(virt_tile * virt_cols, pair_count)
    factors = hole_factors.astype(jnp.float32).reshape(-1, occupied, occupied)
    quadratic = lax.dot_general(
        amp_matrix, ints_matrix, (((0,), (0,)), ((), ())), preferred_element_type=jnp.float32
    )
    pair_index = lax.iota(jnp.int32, pair_count)
    orbital_ids = lax.iota(jnp.int32, occupied)
    first_sel = ((pair_index // occupied)[:, None] == orbital_ids[None, :]).astype(jnp.float32)
    second_sel = ((pair_index % occupied)[:, None] == orbital_ids[None, :]).astype(jnp.float32)
    left_rows = jnp.einsum("ra,pak->prk", first_sel, factors)
    right_rows = jnp.einsum("ra,pal->prl", second_sel, factors)
    density = jnp.einsum("prk,prl->rkl", left_rows, right_rows).reshape(
        pair_count, occupied * occupied
    )
    all_terms = quadratic + density
    hole_part = lax.psum_scatter(all_terms, ("oi", "oj"), scatter_dimension=0, tiled=True).astype(
        jnp.bfloat16
    )
    hole_ints = lax.all_gather(hole_part, ("oi", "oj"), axis=0, tiled=True)
    ladder = lax.dot_general(
        amp_matrix, hole_ints, (((1,), (1,)), ((), ())), preferred_element_type=jnp.float32
    )
    partial_value = (ladder + ints_matrix.astype(jnp.float32)).astype(jnp.bfloat16)
    partial_value = partial_value.reshape(virt_tile, virt_cols, pair_count)
    partial_value = lax.all_to_all(partial_value, "oi", split_axis=2, concat_axis=1, tiled=True)
    tile_occ = partial_value.shape[2] // occupied
    blocks = partial_value.reshape(virt_tile, virtual, tile_occ, occupied)
    mirrored = lax.all_to_all(
        lax.all_to_all(blocks, "oi", split_axis=3, concat_axis=2, tiled=True),
        "oj",
        split_axis=1,
        concat_axis=0,
        tiled=True,
    )
    mirror_part = jnp.transpose(mirrored, (1, 0, 3, 2)).astype(jnp.float32)
    summed_pair = blocks.astype(jnp.float32) + mirror_part
    vir_rows = lax.dynamic_slice_in_dim(vir_energy, lax.axis_index("oj") * virt_tile, virt_tile)
    occ_rows = lax.dynamic_slice_in_dim(occ_energy, lax.axis_index("oi") * tile_occ, tile_occ)
    denominator = (
        vir_rows[:, None, None, None]
        + vir_energy[None, :, None, None]
        - occ_rows[None, None, :, None]
        - occ_energy[None, None, None, :]
    )
    return (summed_pair / denominator).reshape(virt_tile, virtual, tile_occ * occupied)


def solution(mesh):
    placed = (P("oj", "oi", None), P("oj", "oi", None), P(("oi", "oj"), None), P(), P())
    return jax.shard_map(
        local, mesh=mesh, in_specs=placed, out_specs=P("oj", None, "oi"), check_vma=False
    )
```

profile of v0, /device:TPU:1, one launch (start us, length us, event | category | flops | bytes accessed | tf_op | source)
XLA Modules:
  0.0 1028.9 jit_solution(7280143914403209898)
XLA Ops:
  6.5 0.9 reshape.88
  7.6 1.3 fusion.2
  8.8 2.7 copy.45
  11.5 1.3 fusion.3
  12.8 3.5 copy.46
  16.2 8.3 fusion.13
  24.5 11.5 %copy.47 = f32[1024,32,32]{0,2,1:T(8,128)} copy(f32[1024,32,32]{2,1,0:T(8,128)} %fusion.13) | data formatting | bytes 8388608 | tf_op jit(solution)/shard_map/prk,prl->rkl/dot_general | solution.py:23
  36.0 5.4 copy.48
  41.4 5.4 bitcast_add_fusion
  46.9 647.4 %reduce-scatter.2.cloned.1.call-done = f32[8,1024]{1,0:T(8,128)} async-done(((f32[1024,1024]{1,0:T(8,128)}), f32[8,1024]{1,0:T(8,128)}) %reduce-scatter.2.cloned.1.call-update) | async-done | bytes 32784 | tf_op jit(solution)/shard_map/reduce_scatter | solution.py:27
  694.3 1.4 convert_element_type.33
  695.7 196.3 %all-gather.2.cloned.1.call-done = bf16[1024,1024]{1,0:T(8,128)(2,1)} async-done(((bf16[8,1024]{1,0:T(8,128)(2,1)}), bf16[1024,1024]{1,0:T(8,128)(2,1)}) %all-gather.2.cloned.1.call-update) | async-done | bytes 2097168 | tf_op jit(solution)/shard_map/all_gather | solution.py:30
  892.0 2.9 fusion
  894.8 4.8 copy.49
  899.6 7.0 reshape.102
  906.6 17.0 %all_to_all.42 = bf16[8,2,32768]{2,1,0:T(2,128)(2,1)S(1)} all-to-all(bf16[8,2,32768]{2,1,0:T(2,128)(2,1)S(1)} %reshape.102), channel_id=1, replica_groups=mesh['oi'=8,'oj'=16] {'oi'}, dimensions={0} | all-to-all | bytes 2097152 | tf_op jit(solution)/shard_map/all_to_all | solution.py:36
  923.6 4.5 reshape.103
  928.1 6.9 copy.51
  935.0 5.3 reshape.92
  940.3 0.8 copy.52
  941.2 15.5 %all_to_all.43 = bf16[16,256,4,32]{1,2,0,3:T(4,128)(2,1)S(1)} all-to-all(bf16[16,256,4,32]{1,2,0,3:T(4,128)(2,1)S(1)} %copy.52), channel_id=1, replica_groups=mesh['oi'=8,'oj'=16] {'oi'}, dimensions={3} | all-to-all | bytes 2097152 | tf_op jit(solution)/shard_map/all_to_all | solution.py:40
  956.9 6.9 copy.55
  963.8 7.4 reshape.104
  971.2 8.6 all-to-all-start.2
  980.1 16.9 %all-to-all-done.2 = bf16[16,2,16384]{2,1,0:T(2,128)(2,1)S(1)} async-done(((bf16[16,2,16384]{2,1,0:T(2,128)(2,1)}), bf16[16,2,16384]{2,1,0:T(2,128)(2,1)S(1)}, u32[]{:S(2)}, u32[]{:S(2)}) %all-to-all-start.2) | async-done | bytes 1048608 | tf_op jit(solution)/shard_map/all_to_all | solution.py:39
  997.1 3.5 reshape.105
  1000.6 4.9 copy.56
  1005.5 1.1 convert_bitcast_fusion
  1006.6 4.3 copy.57
  1010.9 6.3 copy.58
  1017.2 1.8 fusion.1
  1019.1 3.0 copy.59
  (23 shorter events, 0.8 us)
Async XLA Ops:
  6.5 34.9 %copy-start = (bf16[16,32,1024]{2,1,0:T(8,128)(2,1)S(1)}, bf16[16,32,1024]{2,1,0:T(8,128)(2,1)}, u32[]{:S(2)}) copy-start(bf16[16,32,1024]{2,1,0:T(8,128)(2,1)} %param.5) | copy-start | bytes 3145732
  6.5 687.7 %reduce-scatter.2.cloned.1.call-start = ((), (), s32[]{:S(2)}) async-start(), calls=%async_computation.4 | async-start | bytes 4227072 | tf_op jit(solution)/shard_map/reduce_scatter | solution.py:27
  36.0 5.5 copy-start.4
  46.9 845.1 %all-gather.2.cloned.1.call-start = ((), (), s32[]{:S(2)}) async-start(), calls=%async_computation.5 | async-start | bytes 2113536 | tf_op jit(solution)/shard_map/all_gather | solution.py:30
  971.2 8.6 copy-start.3
  971.2 8.7 copy-start.2
  971.2 25.8 %all-to-all-start.2 = ((bf16[16,2,16384]{2,1,0:T(2,128)(2,1)}), bf16[16,2,16384]{2,1,0:T(2,128)(2,1)S(1)}, u32[]{:S(2)}, u32[]{:S(2)}) async-start(bf16[16,2,16384]{2,1,0:T(2,128)(2,1)} %reshape.104), calls=%async_computation.3 | async-start | bytes 2097152 | tf_op jit(solution)/shard_map/all_to_all | solution.py:39
  1019.1 3.0 copy-start.1
Sparse Core Ops, SparseCore 0:
  47.0 647.2 reduce-scatter.1
  696.0 195.9 all-gather.1
where the time goes:
time: 1030 us
  waiting for transfers between devices  861 us (84%)
  local copies, waits for them, and re-layouts  90 us (9%)
  blocking collectives  32.5 us (3%)
  matrix products  19.1 us (2%)
  between operations  13.5 us (1%)
    reduce_scatter x1, waiting for transfers between devices, local(): lax.psum_scatter(all_terms, ('oi', 'oj'), scatter_dimension=0, tiled=True)  647 us
    all_gather x1, waiting for transfers between devices, local(): hole_ints = lax.all_gather(hole_part, ('oi', 'oj'), axis=0, tiled=True)  196 us
    unnamed x14, local copies, waits for them, and re-layouts  22.5 us
  transfers between devices with their start and end apart: 3, of which 3 were waited for; matrix products, arithmetic and copies ran while one was open for 0% of the time, Pallas kernels for 0%

commit v1 on v0

v1 whole, which is shorter than its diff:
```python
import functools

import jax
import jax.numpy as jnp
from jax import lax
from jax.experimental import pallas as pl
from jax.experimental.pallas import tpu as pltpu
from jax.sharding import Mesh, PartitionSpec as P

BF16, F32 = jnp.bfloat16, jnp.float32
CHIPS = ("x", "y", "zh", "zl")
OI = ("x", "zl")
OJ = ("zh", "y", "c")
ALL = OI + OJ
SWAP = [(0, 1), (1, 0)]
VMEM_LIMIT = 48 * 1024 * 1024


def params():
    return pltpu.CompilerParams(vmem_limit_bytes=VMEM_LIMIT)


def quad_kernel(core, amp_own, amp_peer, ints_own, ints_peer, fac, out, left, right, acc):
    step = pl.program_id(0)

    @pl.when(step == 0)
    def _():
        row = lax.broadcasted_iota(jnp.int32, (32, 1024), 0)
        col = lax.broadcasted_iota(jnp.int32, (32, 1024), 1)
        pick_k = (row == col // 32).astype(F32).astype(BF16)
        pick_l = (row == col % 32).astype(F32).astype(BF16)
        left[...] = jnp.dot(fac[...], pick_k, preferred_element_type=F32)
        right[...] = jnp.dot(fac[...], pick_l, preferred_element_type=F32)

    dims = (((0,), (0,)), ((), ()))
    acc[...] = lax.dot_general(
        amp_own[...], ints_own[...], dims, preferred_element_type=F32
    ) + lax.dot_general(amp_peer[...], ints_peer[...], dims, preferred_element_type=F32)

    def one(ii, carry):
        first = core[0] * 16 + step * 4 + ii
        rows = pl.ds(pl.multiple_of(ii * 32, 32), 32)
        total = acc[rows, :]
        for p in range(16):
            total = total + left[pl.ds(p * 32 + first, 1), :] * right[p * 32 : p * 32 + 32, :]
        out[rows, :] = total.astype(BF16)
        return carry

    lax.fori_loop(0, 4, one, 0)


def sum_kernel(parts, out):
    total = jnp.sum(parts[...].astype(F32), axis=0).astype(BF16)
    out[...] = jnp.broadcast_to(total[None], out.shape)


def ladder_kernel(core, amp, own, peer, ints, out):
    mine = pl.program_id(0) // 4 == core[0]
    rows = jnp.where(mine, own[...], peer[...])
    total = lax.dot_general(
        amp[...], rows, (((1,), (1,)), ((), ())), preferred_element_type=F32
    )
    out[0] = (total + ints[...].astype(F32)).astype(BF16)


def spread_kernel(part, perm, out, wide):
    for r in range(8):
        for ob in range(2):
            for ah in range(2):
                base = ((r * 2 + ob) * 2 + ah) * 16
                for al in range(8):
                    wide[base : base + 16, al * 128 : al * 128 + 128] = part[
                        r, ah * 8 + al, ob * 16 : ob * 16 + 16, :
                    ]
    for q in range(8):
        moved = jnp.dot(
            wide[...], perm[:, q * 128 : q * 128 + 128], preferred_element_type=F32
        )
        out[q] = moved.astype(BF16).reshape(16, 32, 128)


def final_kernel(place, occ, vir, part, mirror, perm, virb, out, wide):
    for q in range(8):
        wide[:, q * 128 : q * 128 + 128] = mirror[q].reshape(512, 128)
    for al in range(8):
        moved = jnp.dot(
            wide[...], perm[:, al * 128 : al * 128 + 128], preferred_element_type=F32
        )
        for o in range(16):
            for ah in range(2):
                base = (o * 2 + ah) * 16
                out[pl.ds(o * 16 + ah * 8 + al, 16, stride=256), :] = moved[base : base + 16, :]
    lane = lax.broadcasted_iota(jnp.int32, (8, 128), 1)
    first = jnp.zeros((8, 128), F32)
    second = jnp.zeros((8, 128), F32)
    for i in range(4):
        first = jnp.where(lane // 32 == i, occ[place[0] * 4 + i], first)
    for j in range(32):
        second = jnp.where(lane % 32 == j, occ[j], second)
    first, second = first[:1], second[:1]

    def one(a, carry):
        energy = vir[place[1] * 16 + a]
        for r in range(8):
            rows = pl.ds(pl.multiple_of(a * 256 + r * 32, 32), 32)
            direct = part[r, pl.ds(pl.multiple_of(a * 32, 32), 32), :].astype(F32)
            low = energy + virb[r * 32 : r * 32 + 32, :] - first - second
            out[rows, :] = (direct + out[rows, :]) / low
        return carry

    lax.fori_loop(0, 16, one, 0)


def moves():
    row = lax.broadcasted_iota(jnp.int32, (1024, 1024), 0)
    col = lax.broadcasted_iota(jnp.int32, (1024, 1024), 1)
    high, mid, low = row // 128, row % 128, row % 4
    spread = (mid // 4 % 8) * 128 + high * 16 + (mid // 32) * 4 + low
    gather = (mid // 16) * 128 + low * 32 + high * 4 + mid // 4 % 4
    return (spread == col).astype(BF16), (gather == col).astype(BF16)


def swap_chips(value):
    return lax.all_to_all(value, CHIPS, 0, 0, tiled=False)


def local(amplitudes, exchange_ints, hole_factors, occ_energy, vir_energy):
    core = lax.axis_index("c").astype(jnp.int32).reshape(1)
    place = jnp.stack([lax.axis_index(OI), lax.axis_index(OJ)]).astype(jnp.int32)
    amp = amplitudes.reshape(512, 1024)
    ints = exchange_ints.reshape(512, 1024)
    amp_peer = lax.ppermute(amp, "c", SWAP)
    ints_peer = lax.ppermute(ints, "c", SWAP)
    fac_peer = lax.ppermute(hole_factors, "c", SWAP)
    spread, gather = moves()
    virb = jnp.broadcast_to(vir_energy[:, None], (256, 128))
    factors = jnp.concatenate([hole_factors, fac_peer]).reshape(512, 32)
    whole = lambda shape: pl.BlockSpec(shape, lambda g, s: (0,) * len(shape))
    half_part = pl.pallas_call(
        quad_kernel,
        out_shape=jax.ShapeDtypeStruct((512, 1024), BF16),
        grid_spec=pltpu.PrefetchScalarGridSpec(
            num_scalar_prefetch=1,
            grid=(4,),
            in_specs=[
                pl.BlockSpec((512, 128), lambda g, s: (0, s[0] * 4 + g)),
                pl.BlockSpec((512, 128), lambda g, s: (0, s[0] * 4 + g)),
                whole((512, 1024)),
                whole((512, 1024)),
                whole((512, 32)),
            ],
            out_specs=pl.BlockSpec((128, 1024), lambda g, s: (g, 0)),
            scratch_shapes=[
                pltpu.VMEM((512, 1024), F32),
                pltpu.VMEM((512, 1024), F32),
                pltpu.VMEM((128, 1024), F32),
            ],
        ),
        compiler_params=params(),
        name="quad",
    )(core, amp, amp_peer, ints, ints_peer, factors)
    parts = swap_chips(half_part.reshape(64, 8, 1024))
    vmem = pl.BlockSpec(memory_space=pltpu.VMEM)
    smem = pl.BlockSpec(memory_space=pltpu.SMEM)
    sent = pl.pallas_call(
        sum_kernel,
        out_shape=jax.ShapeDtypeStruct((64, 8, 1024), BF16),
        in_specs=[vmem],
        out_specs=vmem,
        compiler_params=params(),
        name="sum",
    )(parts)
    hole_own = swap_chips(sent).reshape(512, 1024)
    hole_peer = lax.ppermute(hole_own, "c", SWAP)
    chunks = pl.pallas_call(
        ladder_kernel,
        out_shape=jax.ShapeDtypeStruct((8, 512, 128), BF16),
        grid_spec=pltpu.PrefetchScalarGridSpec(
            num_scalar_prefetch=1,
            grid=(8,),
            in_specs=[
                whole((512, 1024)),
                pl.BlockSpec((128, 1024), lambda g, s: (g % 4, 0)),
                pl.BlockSpec((128, 1024), lambda g, s: (g % 4, 0)),
                pl.BlockSpec((512, 128), lambda g, s: (0, g)),
            ],
            out_specs=pl.BlockSpec((1, 512, 128), lambda g, s: (g, 0, 0)),
        ),
        compiler_params=params(),
        name="ladder",
    )(core, amp, hole_own, hole_peer, ints)
    part = lax.all_to_all(chunks, OI, 0, 0, tiled=False)
    outgoing = pl.pallas_call(
        spread_kernel,
        out_shape=jax.ShapeDtypeStruct((8, 16, 32, 128), BF16),
        in_specs=[vmem, vmem],
        out_specs=vmem,
        scratch_shapes=[pltpu.VMEM((512, 1024), BF16)],
        compiler_params=params(),
        name="spread",
    )(part.reshape(8, 16, 32, 128), spread)
    mirror = lax.all_to_all(outgoing.reshape(128, 32, 128), ALL, 0, 0, tiled=False)
    result = pl.pallas_call(
        final_kernel,
        out_shape=jax.ShapeDtypeStruct((4096, 128), F32),
        in_specs=[smem, smem, smem, vmem, vmem, vmem, vmem],
        out_specs=vmem,
        scratch_shapes=[pltpu.VMEM((512, 1024), BF16)],
        compiler_params=params(),
        name="final",
    )(place, occ_energy, vir_energy, part, mirror.reshape(8, 16, 32, 128), gather, virb)
    return result.reshape(16, 256, 128)


def solution(mesh):
    fine = Mesh(mesh.devices.reshape(4, 2, 2, 4, 2), ALL)
    placed = (P(OJ, OI, None), P(OJ, OI, None), P(ALL, None), P(), P())
    return jax.shard_map(
        local, mesh=fine, in_specs=placed, out_specs=P(OJ, None, OI), check_vma=False
    )
```

time: 1030 us -> 132 us (0.13)
  waiting for transfers between devices: 861 us -> 35.6 us
  local copies, waits for them, and re-layouts: 90 us -> 5.25 us
  Pallas kernels: 0 us -> 20.3 us
  matrix products: 19.1 us -> 0 us
  blocking collectives: 32.5 us -> 49.6 us
  between operations: 13.5 us -> 0.14 us
    reduce_scatter x1 -> x0, waiting for transfers between devices: 647 us -> none  [local(): lax.psum_scatter(all_terms, ('oi', 'oj'), scatter_dimension=0, tiled=True)]
    all_gather x1 -> x0, waiting for transfers between devices: 196 us -> none  [local(): hole_ints = lax.all_gather(hole_part, ('oi', 'oj'), axis=0, tiled=True)]
    pallas_call x0 -> x5, Pallas kernels: none -> 20.3 us  [the longest x1 6.47 us: local(): pl.pallas_call(final_kernel, out_shape=jax.ShapeDtypeStruct((4096, 128),...]
    reshape x7 -> x1, local copies, waits for them, and re-layouts: 20.4 us -> 0.15 us  [local(): factors = jnp.concatenate([hole_factors, fac_peer]).reshape(512, 32)]
    all_to_all x5 -> x0, local copies, waits for them, and re-layouts: 18.9 us -> none  [the longest x3 7.14 us: local(): lax.all_to_all(blocks, 'oi', split_axis=3, concat_axis=2, tiled=True)]
    unnamed x14 -> x16, local copies, waits for them, and re-layouts: 22.5 us -> 5.01 us
    all_to_all x2, blocking collectives: 32.5 us -> 49.6 us  [swap_chips(): return lax.all_to_all(value, CHIPS, 0, 0, tiled=False)]
    dot_general x3 -> x0, matrix products: 16.6 us -> none  [the longest x1 8.27 us: local(): jnp.einsum('prk,prl->rkl', left_rows, right_rows)]
  transfers between devices with their start and end apart: 3 -> 6, of which waited for: 3 -> 4; matrix products, arithmetic and copies ran while one was open for 0% -> 4% of each run, Pallas kernels for 0% -> 0%
where the time goes in v1:
time: 132 us; the launch traced here: 131 us
  blocking collectives  49.6 us (38%)
  waiting for transfers between devices  35.6 us (27%)
  Pallas kernels  20.3 us (15%)
  starting transfers between devices  14.5 us (11%)
  other arithmetic  5.63 us (4%)
  local copies, waits for them, and re-layouts  5.25 us (4%)
    all_to_all x2, blocking collectives, swap_chips(): return lax.all_to_all(value, CHIPS, 0, 0, tiled=False)  49.6 us
    all_to_all x1, waiting for transfers between devices, local(): lax.all_to_all(outgoing.reshape(128, 32, 128), ALL, 0, 0, tiled=False)  18.5 us
    all_to_all x1, waiting for transfers between devices, local(): part = lax.all_to_all(chunks, OI, 0, 0, tiled=False)  11.3 us
    pallas_call x1, Pallas kernels, local(): pl.pallas_call(final_kernel, out_shape=jax.ShapeDtypeStruct((4096, 128),...  6.47 us
    pallas_call x1, Pallas kernels, local(): pl.pallas_call(quad_kernel, out_shape=jax.ShapeDtypeStruct((512, 1024), B...  6.18 us
    all_to_all x1, starting transfers between devices, local(): lax.all_to_all(outgoing.reshape(128, 32, 128), ALL, 0, 0, tiled=False)  5.86 us
    pallas_call x1, Pallas kernels, local(): pl.pallas_call(ladder_kernel, out_shape=jax.ShapeDtypeStruct((8, 512, 128...  5.09 us
    unnamed x16, local copies, waits for them, and re-layouts  5.01 us
  transfers between devices with their start and end apart: 6, of which 4 were waited for; matrix products, arithmetic and copies ran while one was open for 4% of the time, Pallas kernels for 0%

profile of v1, /device:TPU:1, one launch (start us, length us, event | category | flops | bytes accessed | tf_op | source)
XLA Modules:
  0.0 131.1 jit_solution(12284412457664946889)
XLA Ops:
  0.0 1.4 %collective-permute-start = (bf16[512,1024]{1,0:T(8,128)(2,1)}, bf16[512,1024]{1,0:T(8,128)(2,1)S(1)}, u32[]{:S(2)}, u32[]{:S(2)}) collective-permute-start(bf16[512,1024]{1,0:T(8,128)(2,1)} %bitcast.16), channel_id=1, source_target_pairs={{0,1},{1,0},{2,3},{3,2},{4,5},{5,4},{6,7},{7,6},{8,9},{9,8},{10,11... | collective-permute-start | bytes 3145736 | tf_op jit(solution)/shard_map/ppermute | solution.py:132
  1.4 0.0 collective-permute-start.1
  1.4 0.5 collective-permute-start.2
  1.9 3.5 %collective-permute-done.2 = bf16[8,1024]{1,0:T(8,128)(2,1)S(1)} collective-permute-done((bf16[8,1024]{1,0:T(8,128)(2,1)}, bf16[8,1024]{1,0:T(8,128)(2,1)S(1)}, u32[]{:S(2)}, u32[]{:S(2)}) %collective-permute-start.2) | collective-permute-done | bytes 16416 | tf_op jit(solution)/shard_map/ppermute | solution.py:134
  5.4 0.7 pad_maximum_fusion
  6.1 0.1 reshape.34.fac
  6.3 0.0 collective-permute-done.amp_peer
  6.3 0.0 collective-permute-done.1.ints_peer
  6.3 0.0 copy-start.2
  6.3 1.2 copy-done.2
  7.5 1.2 copy-done.4
  8.8 6.2 %quad.1 = bf16[512,1024]{1,0:T(8,128)(2,1)S(1)} custom-call(s32[1]{0:T(128)} %bitcast.2.core, bf16[512,1024]{1,0:T(8,128)(2,1)S(1)} %bitcast.17, bf16[512,1024]{1,0:T(8,128)(2,1)S(1)} %collective-permute-done.amp_peer, bf16[512,1024]{1,0:T(8,128)(2,1)S(1)} %bitcast.20, bf16[512,1024]{1,0:T(8,128)(2,1)S(1)} %collective-permute-done.1.ints_peer, ...), custom_call_target="tpu_custom_call" | custom-call | tf_op jit(solution)/shard_map/quad/pallas_call | solution.py:139
  14.9 27.9 %all_to_all.20.parts = bf16[64,8,1024]{2,1,0:T(8,128)(2,1)S(1)} all-to-all(bf16[64,8,1024]{2,1,0:T(8,128)(2,1)S(1)} %bitcast.15), channel_id=1, replica_groups=mesh['x'=4,'zl'=2,'zh'=2,'y'=4,'c'=2] {'x','y','zh','zl'}, dimensions={0} | all-to-all | bytes 2097152 | tf_op jit(solution)/shard_map/all_to_all | solution.py:124
  42.9 0.2 sum.1
  43.1 21.7 %all_to_all.21 = bf16[64,8,1024]{2,1,0:T(8,128)(2,1)S(1)} all-to-all(bf16[64,8,1024]{2,1,0:T(8,128)(2,1)S(1)} %sum.1), channel_id=1, replica_groups=mesh['x'=4,'zl'=2,'zh'=2,'y'=4,'c'=2] {'x','y','zh','zl'}, dimensions={0} | all-to-all | bytes 2097152 | tf_op jit(solution)/shard_map/all_to_all | solution.py:124
  64.8 3.2 %collective-permute-start.3 = (bf16[512,1024]{1,0:T(8,128)(2,1)S(1)}, bf16[512,1024]{1,0:T(8,128)(2,1)S(1)}, u32[]{:S(2)}, u32[]{:S(2)}) collective-permute-start(bf16[512,1024]{1,0:T(8,128)(2,1)S(1)} %bitcast.13), channel_id=1, source_target_pairs={{0,1},{1,0},{2,3},{3,2},{4,5},{5,4},{6,7},{7,6},{8,9},{9,8},{10,11... | collective-permute-start | bytes 3145736 | tf_op jit(solution)/shard_map/ppermute | solution.py:174
  68.1 2.2 %collective-permute-done.3.peer = bf16[512,1024]{1,0:T(8,128)(2,1)S(1)} collective-permute-done((bf16[512,1024]{1,0:T(8,128)(2,1)S(1)}, bf16[512,1024]{1,0:T(8,128)(2,1)S(1)}, u32[]{:S(2)}, u32[]{:S(2)}) %collective-permute-start.3) | collective-permute-done | bytes 1048608 | tf_op jit(solution)/shard_map/ppermute | solution.py:174
  70.3 0.0 copy-done.3
  70.3 5.1 %ladder.1 = bf16[8,512,128]{2,1,0:T(8,128)(2,1)} custom-call(s32[1]{0:T(128)} %bitcast.2.core, bf16[512,1024]{1,0:T(8,128)(2,1)S(1)} %bitcast.18, bf16[512,1024]{1,0:T(8,128)(2,1)S(1)} %bitcast.14, bf16[512,1024]{1,0:T(8,128)(2,1)S(1)} %collective-permute-done.3.peer, bf16[512,1024]{1,0:T(8,128)(2,1)S(1)} %bitcast.21), custom_call_target="tpu_custom_call" | custom-call | tf_op jit(solution)/shard_map/ladder/pallas_call | solution.py:175
  75.4 3.6 %all-to-all-start.2 = ((bf16[8,512,128]{2,1,0:T(8,128)(2,1)}), bf16[8,512,128]{2,1,0:T(8,128)(2,1)S(1)}, u32[]{:S(2)}, u32[]{:S(2)}) async-start(bf16[8,512,128]{2,1,0:T(8,128)(2,1)} %ladder.1), calls=%async_computation.2 | async-start | bytes 2097152 | tf_op jit(solution)/shard_map/all_to_all | solution.py:192
  79.0 4.8 %fusion.24 = (bf16[1024,1024]{1,0:T(8,128)(2,1)S(1)}, bf16[1024,1024]{1,0:T(8,128)(2,1)}) fusion(s32[1024]{0:T(1024)S(1)} %get-tuple-element.7, s32[1024]{0:T(1024)S(1)} %get-tuple-element.11, s32[1024]{0:T(1024)S(1)} %get-tuple-element.8, s32[1024]{0:T(1024)S(1)} %get-tuple-element.12, s32[1024]{0:T(1024)S(1)} %get-tuple-element.9, ...), kind=kLoop, calls=%fused_computation.46 | loop fusion | flops 76546048 | bytes 4221952 | tf_op jit(solution)/shard_map/convert_element_type | solution.py:120
  83.8 11.3 %all-to-all-done.2.part = bf16[8,512,128]{2,1,0:T(8,128)(2,1)S(1)} async-done(((bf16[8,512,128]{2,1,0:T(8,128)(2,1)}), bf16[8,512,128]{2,1,0:T(8,128)(2,1)S(1)}, u32[]{:S(2)}, u32[]{:S(2)}) %all-to-all-start.2) | async-done | bytes 1048608 | tf_op jit(solution)/shard_map/all_to_all | solution.py:192
  95.1 1.6 %copy-done = bf16[1024,1024]{1,0:T(8,128)(2,1)S(1)} copy-done((bf16[1024,1024]{1,0:T(8,128)(2,1)S(1)}, bf16[1024,1024]{1,0:T(8,128)(2,1)}, u32[]{:S(2)}) %copy-start) | copy-done | bytes 2097176
  96.7 2.3 %spread.1 = bf16[8,16,32,128]{3,2,1,0:T(8,128)(2,1)S(1)} custom-call(bf16[8,16,32,128]{3,2,1,0:T(8,128)(2,1)S(1)} %bitcast.11, bf16[1024,1024]{1,0:T(8,128)(2,1)S(1)} %copy-done), custom_call_target="tpu_custom_call" | custom-call | tf_op jit(solution)/shard_map/spread/pallas_call | solution.py:193
  99.1 0.0 copy-start.1
  99.1 1.0 copy-done.1
  100.1 5.9 %all-to-all-start.3 = ((bf16[128,32,128]{2,1,0:T(8,128)(2,1)}), bf16[128,32,128]{2,1,0:T(8,128)(2,1)}, u32[]{:S(2)}, u32[]{:S(2)}) async-start(bf16[128,32,128]{2,1,0:T(8,128)(2,1)} %bitcast.12), calls=%async_computation.3 | async-start | bytes 2097152 | tf_op jit(solution)/shard_map/all_to_all | solution.py:202
  105.9 0.1 pad_add_fusion.place
  106.0 18.5 %all-to-all-done.3 = bf16[128,32,128]{2,1,0:T(8,128)(2,1)} async-done(((bf16[128,32,128]{2,1,0:T(8,128)(2,1)}), bf16[128,32,128]{2,1,0:T(8,128)(2,1)}, u32[]{:S(2)}, u32[]{:S(2)}) %all-to-all-start.3) | async-done | bytes 1048608 | tf_op jit(solution)/shard_map/all_to_all | solution.py:202
  124.5 0.1 broadcast_in_dim.2.virb
  124.6 0.0 copy-done.7
  124.6 6.5 %final.1 = f32[4096,128]{1,0:T(8,128)} custom-call(s32[2]{0:T(128)S(1)} %pad_add_fusion.place, f32[32]{0:T(128)S(1)} %copy-done.7, f32[256]{0:T(256)S(1)} %copy-done.6, bf16[8,512,128]{2,1,0:T(8,128)(2,1)S(1)} %all-to-all-done.2.part, bf16[8,16,32,128]{3,2,1,0:T(8,128)(2,1)} %bitcast.9.mirror, bf16[1024,1024]{1,0:T(8,128)(2,1)S(1)} %get-tuple-element.5.perm, ...), custom_call_target="tpu_custom_call" | custom-call | tf_op jit(solution)/shard_map/final/pallas_call | solution.py:203
  (13 shorter events, 0.0 us)
Async XLA Ops:
  0.0 6.3 %collective-permute-start = (bf16[512,1024]{1,0:T(8,128)(2,1)}, bf16[512,1024]{1,0:T(8,128)(2,1)S(1)}, u32[]{:S(2)}, u32[]{:S(2)}) collective-permute-start(bf16[512,1024]{1,0:T(8,128)(2,1)} %bitcast.16), channel_id=1, source_target_pairs={{0,1},{1,0},{2,3},{3,2},{4,5},{5,4},{6,7},{7,6},{8,9},{9,8},{10,11... | collective-permute-start | bytes 3145736 | tf_op jit(solution)/shard_map/ppermute | solution.py:132
  1.4 4.9 %collective-permute-start.1 = (bf16[512,1024]{1,0:T(8,128)(2,1)}, bf16[512,1024]{1,0:T(8,128)(2,1)S(1)}, u32[]{:S(2)}, u32[]{:S(2)}) collective-permute-start(bf16[512,1024]{1,0:T(8,128)(2,1)} %bitcast.19), channel_id=1, source_target_pairs={{0,1},{1,0},{2,3},{3,2},{4,5},{5,4},{6,7},{7,6},{8,9},{9,8},{10,11... | collective-permute-start | bytes 3145736 | tf_op jit(solution)/shard_map/ppermute | solution.py:133
  1.4 4.0 %collective-permute-start.2 = (bf16[8,1024]{1,0:T(8,128)(2,1)}, bf16[8,1024]{1,0:T(8,128)(2,1)S(1)}, u32[]{:S(2)}, u32[]{:S(2)}) collective-permute-start(bf16[8,1024]{1,0:T(8,128)(2,1)} %param.7), channel_id=1, source_target_pairs={{0,1},{1,0},{2,3},{3,2},{4,5},{5,4},{6,7},{7,6},{8,9},{9,8},{10,11... | collective-permute-start | bytes 49160 | tf_op jit(solution)/shard_map/ppermute | solution.py:134
  6.3 1.2 copy-start.2
  7.5 1.2 copy-start.4
  42.9 27.5 %copy-start.3 = (bf16[16,32,1024]{2,1,0:T(8,128)(2,1)S(1)}, bf16[16,32,1024]{2,1,0:T(8,128)(2,1)}, u32[]{:S(2)}) copy-start(bf16[16,32,1024]{2,1,0:T(8,128)(2,1)} %param.5) | copy-start | bytes 3145732
  42.9 27.5 %copy-start.5 = (bf16[16,32,1024]{2,1,0:T(8,128)(2,1)S(1)}, bf16[16,32,1024]{2,1,0:T(8,128)(2,1)}, u32[]{:S(2)}) copy-start(bf16[16,32,1024]{2,1,0:T(8,128)(2,1)} %param.6) | copy-start | bytes 3145732
  64.8 5.5 %collective-permute-start.3 = (bf16[512,1024]{1,0:T(8,128)(2,1)S(1)}, bf16[512,1024]{1,0:T(8,128)(2,1)S(1)}, u32[]{:S(2)}, u32[]{:S(2)}) collective-permute-start(bf16[512,1024]{1,0:T(8,128)(2,1)S(1)} %bitcast.13), channel_id=1, source_target_pairs={{0,1},{1,0},{2,3},{3,2},{4,5},{5,4},{6,7},{7,6},{8,9},{9,8},{10,11... | collective-permute-start | bytes 3145736 | tf_op jit(solution)/shard_map/ppermute | solution.py:174
  75.4 19.7 %all-to-all-start.2 = ((bf16[8,512,128]{2,1,0:T(8,128)(2,1)}), bf16[8,512,128]{2,1,0:T(8,128)(2,1)S(1)}, u32[]{:S(2)}, u32[]{:S(2)}) async-start(bf16[8,512,128]{2,1,0:T(8,128)(2,1)} %ladder.1), calls=%async_computation.2 | async-start | bytes 2097152 | tf_op jit(solution)/shard_map/all_to_all | solution.py:192
  95.1 1.6 %copy-start = (bf16[1024,1024]{1,0:T(8,128)(2,1)S(1)}, bf16[1024,1024]{1,0:T(8,128)(2,1)}, u32[]{:S(2)}) copy-start(bf16[1024,1024]{1,0:T(8,128)(2,1)} %get-tuple-element.6.perm) | copy-start | bytes 6291460
  99.1 1.0 copy-start.1
  100.1 24.4 %copy-start.6 = (f32[256]{0:T(256)S(1)}, f32[256]{0:T(256)}, u32[]{:S(2)}) copy-start(f32[256]{0:T(256)} %vir.1) | copy-start | bytes 3076
  100.1 24.5 %copy-start.7 = (f32[32]{0:T(128)S(1)}, f32[32]{0:T(128)}, u32[]{:S(2)}) copy-start(f32[32]{0:T(128)} %occ.1) | copy-start | bytes 388
  100.1 24.4 %all-to-all-start.3 = ((bf16[128,32,128]{2,1,0:T(8,128)(2,1)}), bf16[128,32,128]{2,1,0:T(8,128)(2,1)}, u32[]{:S(2)}, u32[]{:S(2)}) async-start(bf16[128,32,128]{2,1,0:T(8,128)(2,1)} %bitcast.12), calls=%async_computation.3 | async-start | bytes 2097152 | tf_op jit(solution)/shard_map/all_to_all | solution.py:202

commit v2 on v0

v2 whole, which is shorter than its diff:
```python
import jax
import jax.numpy as jnp
from jax import lax
from jax.experimental import pallas as pl
from jax.experimental.pallas import tpu as pltpu
from jax.sharding import Mesh, PartitionSpec as P

BF16, F32 = jnp.bfloat16, jnp.float32
CHIPS = ("x", "y", "zh", "zl")
OI = ("x", "zl")
OJ = ("zh", "y", "c")
ALL = OI + OJ
SWAP = [(0, 1), (1, 0)]
VMEM = pl.BlockSpec(memory_space=pltpu.VMEM)
SMEM = pl.BlockSpec(memory_space=pltpu.SMEM)
ANY = pl.BlockSpec(memory_space=pl.ANY)


def call(kernel, name, outs, ins, out_specs=None, scratch=(), alias=None):
    return pl.pallas_call(
        kernel,
        out_shape=outs,
        in_specs=ins,
        out_specs=out_specs or jax.tree.map(lambda _: VMEM, outs),
        scratch_shapes=list(scratch),
        input_output_aliases=alias or {},
        compiler_params=pltpu.CompilerParams(vmem_limit_bytes=16 * 1024 * 1024),
        name=name,
    )


def shape(dims, dtype=BF16):
    return jax.ShapeDtypeStruct(dims, dtype)


def tables_kernel(place, vir, occ, spread, gather, virb, vira, occ_lanes):
    row = lax.broadcasted_iota(jnp.int32, (128, 128), 0)
    lane = lax.broadcasted_iota(jnp.int32, (128, 128), 1)

    def ones(mask):
        return mask.astype(F32).astype(BF16)

    out_ones = ones(lane % 16 == (row // 32) * 4 + row % 4)
    in_ones = ones(((lane // 32) == row % 4) & (lane % 4 == row // 4 % 4))
    out_rows = [out_ones * ones(row // 4 % 8 == b) for b in range(8)]
    in_rows = [in_ones * ones(row // 16 == b) for b in range(8)]
    for high in range(8):
        rows = slice(high * 128, high * 128 + 128)
        out_lanes = ones(lane // 16 == high)
        in_lanes = ones(lane // 4 % 8 == high)
        for b in range(8):
            cols = slice(b * 128, b * 128 + 128)
            spread[rows, cols] = out_rows[b] * out_lanes
            gather[rows, cols] = in_rows[b] * in_lanes
    for half in range(2):
        cols = slice(half * 128, half * 128 + 128)
        diagonal = jnp.where(row == lane, jnp.broadcast_to(vir[:1, cols], (128, 128)), 0.0)
        virb[cols, :] = jnp.broadcast_to(jnp.sum(diagonal, axis=1, keepdims=True), (128, 128))
    vira[...] = virb[pl.ds(pl.multiple_of(place[1] * 16, 16), 16), :]
    second = occ[...]
    one = lane[:8]
    first = jnp.zeros((8, 128), F32)
    for i in range(4):
        mine = jnp.where(one == place[0] * 4 + i, second, 0.0)
        value = jnp.broadcast_to(jnp.sum(mine, axis=1, keepdims=True), (8, 128))
        first = jnp.where(one // 32 == i, value, first)
    occ_lanes[:8] = first
    occ_lanes[8:] = second


def add_density(core, fac, left, right, start, out):
    row = lax.broadcasted_iota(jnp.int32, (32, 1024), 0)
    col = lax.broadcasted_iota(jnp.int32, (32, 1024), 1)
    pick_k = (row == col // 32).astype(F32).astype(BF16)
    pick_l = (row == col % 32).astype(F32).astype(BF16)
    left[...] = jnp.dot(fac[...], pick_k, preferred_element_type=F32)
    right[...] = jnp.dot(fac[...], pick_l, preferred_element_type=F32)

    def one(i, carry):
        first = core[0] * 16 + i
        rows = pl.ds(pl.multiple_of(i * 32, 32), 32)
        total = left[pl.ds(first, 1), :] * right[:32, :]
        for p in range(1, 8):
            total = total + left[pl.ds(p * 32 + first, 1), :] * right[p * 32 : p * 32 + 32, :]
        out[rows, :] = total if start is None else total + start[rows, :]
        return carry

    lax.fori_loop(0, 16, one, 0)


def quadratic(core, g, amp, ints):
    cols = pl.ds(pl.multiple_of(core[0] * 512 + g * 128, 128), 128)
    return lax.dot_general(
        amp[:, cols], ints[...], (((0,), (0,)), ((), ())), preferred_element_type=F32
    )


def density_kernel(core, fac, out, left, right):
    add_density(core, fac, left, right, None, out)


def own_kernel(core, start, fac, amp, ints, out, left, right, held):
    for g in range(4):
        rows = slice(g * 128, g * 128 + 128)
        held[rows, :] = start[rows, :] + quadratic(core, g, amp, ints)
    add_density(core, fac, left, right, held, out)


def peer_kernel(core, start, amp, ints, out):
    for g in range(4):
        rows = slice(g * 128, g * 128 + 128)
        out[rows, :] = (start[rows, :] + quadratic(core, g, amp, ints)).astype(BF16)


def sum_kernel(parts, out):
    total = jnp.sum(parts[...].astype(F32), axis=0).astype(BF16)
    out[...] = jnp.broadcast_to(total[None], out.shape)


def ladder_kernel(half, amp, hole, ints, *refs):
    out = refs[-1]
    for g in range(2):
        cols = pl.ds(pl.multiple_of(half[0] * 512 + g * 256, 256), 256)
        total = lax.dot_general(
            amp[...],
            hole[g * 256 : g * 256 + 256, :],
            (((1,), (1,)), ((), ())),
            preferred_element_type=F32,
        )
        total = (total + ints[:, cols].astype(F32)).astype(BF16)
        out[half[0] * 4 + g * 2] = total[:, :128]
        out[half[0] * 4 + g * 2 + 1] = total[:, 128:]


def spread_kernel(part, perm, out, wide):
    for r in range(8):
        for ob in range(2):
            for ah in range(2):
                base = ((r * 2 + ob) * 2 + ah) * 16
                for al in range(8):
                    wide[base : base + 16, al * 128 : al * 128 + 128] = part[
                        r, ah * 8 + al, ob * 16 : ob * 16 + 16, :
                    ]
    for q in range(0, 8, 2):
        moved = jnp.dot(
            wide[...], perm[:, q * 128 : q * 128 + 256], preferred_element_type=F32
        ).astype(BF16)
        out[q] = moved[:, :128].reshape(16, 32, 128)
        out[q + 1] = moved[:, 128:].reshape(16, 32, 128)


def final_kernel(part, mirror, perm, virb, vira, occ_lanes, out, wide, held, sems):
    first, second = occ_lanes[:1], occ_lanes[8:9]

    def copy(a, half):
        rows = pl.ds(pl.multiple_of(a * 256 + half * 128, 128), 128)
        return pltpu.make_async_copy(held.at[rows], out.at[rows], sems.at[half * 16 + a])

    for half in range(2):
        mine = slice(half * 256, half * 256 + 256)
        for q in range(8):
            wide[mine, q * 128 : q * 128 + 128] = mirror[q, half * 8 : half * 8 + 8].reshape(256, 128)
        for al in range(0, 8, 2):
            moved = jnp.dot(
                wide[mine, :], perm[:, al * 128 : al * 128 + 256], preferred_element_type=F32
            )
            for o in range(8):
                for ah in range(2):
                    base = (o * 2 + ah) * 16
                    for s in range(2):
                        row = (half * 8 + o) * 16 + ah * 8 + al + s
                        held[pl.ds(row, 16, stride=256), :] = moved[
                            base : base + 16, s * 128 : s * 128 + 128
                        ]

        def one(a, carry):
            energy = vira[pl.ds(a, 1), :]
            for r in range(half * 4, half * 4 + 4):
                rows = pl.ds(pl.multiple_of(a * 256 + r * 32, 32), 32)
                direct = part[r, pl.ds(pl.multiple_of(a * 32, 32), 32), :].astype(F32)
                low = energy + virb[r * 32 : r * 32 + 32, :] - first - second
                held[rows, :] = (direct + held[rows, :]) / low
            copy(a, half).start()
            return carry

        lax.fori_loop(0, 16, one, 0)
    for half in range(2):
        for a in range(16):
            copy(a, half).wait()


def local(amplitudes, exchange_ints, hole_factors, occ_energy, vir_energy):
    core = lax.axis_index("c").astype(jnp.int32).reshape(1)
    place = jnp.stack([lax.axis_index(OI), lax.axis_index(OJ)]).astype(jnp.int32)
    amp = amplitudes.reshape(512, 1024)
    ints = exchange_ints.reshape(512, 1024)
    fac = hole_factors.reshape(256, 32)
    fac_peer = lax.ppermute(fac, "c", SWAP)
    amp_peer = lax.ppermute(amp, "c", SWAP)
    ints_peer = lax.ppermute(ints, "c", SWAP)
    pieces = [pltpu.VMEM((256, 1024), F32)] * 2
    square = shape((512, 1024), F32)
    density = call(density_kernel, "density", square, [SMEM, VMEM], scratch=pieces)(core, fac)
    own = call(own_kernel, "own", square, [SMEM] + [VMEM] * 4, scratch=pieces + [pltpu.VMEM((512, 1024), F32)])(
        core, density, fac_peer, amp, ints
    )
    half_part = call(peer_kernel, "peer", shape((512, 1024)), [SMEM] + [VMEM] * 3)(
        core, own, amp_peer, ints_peer
    )
    parts = lax.all_to_all(half_part.reshape(64, 8, 1024), CHIPS, 0, 0, tiled=False)
    sent = call(sum_kernel, "sum", shape((64, 8, 1024)), [VMEM])(parts)
    hole_own = lax.all_to_all(sent, CHIPS, 0, 0, tiled=False).reshape(512, 1024)
    hole_peer = lax.ppermute(hole_own, "c", SWAP)
    chunks = call(ladder_kernel, "ladder_own", shape((8, 512, 128)), [SMEM] + [VMEM] * 3)(
        core, amp, hole_own, ints
    )
    vir_row = jnp.broadcast_to(vir_energy[None], (8, 256))
    occ_row = jnp.broadcast_to(jnp.tile(occ_energy, 4)[None], (8, 128))
    place, hole_own = lax.optimization_barrier((place, hole_own))
    tables = call(
        tables_kernel,
        "tables",
        (
            shape((1024, 1024)),
            shape((1024, 1024)),
            shape((256, 128), F32),
            shape((16, 128), F32),
            shape((16, 128), F32),
        ),
        [SMEM, VMEM, VMEM],
    )(place, vir_row, occ_row)
    chunks, spread, gather, virb, vira, occ_lanes = lax.optimization_barrier((chunks, *tables))
    chunks = call(
        ladder_kernel, "ladder_peer", shape((8, 512, 128)), [SMEM] + [VMEM] * 4, alias={4: 0}
    )(1 - core, amp, hole_peer, ints, chunks)
    part = lax.all_to_all(chunks, OI, 0, 0, tiled=False)
    outgoing = call(
        spread_kernel,
        "spread",
        shape((8, 16, 32, 128)),
        [VMEM] * 2,
        scratch=[pltpu.VMEM((512, 1024), BF16)],
    )(part.reshape(8, 16, 32, 128), spread)
    mirror = lax.all_to_all(outgoing.reshape(128, 32, 128), ALL, 0, 0, tiled=False)
    result = call(
        final_kernel,
        "final",
        shape((4096, 128), F32),
        [VMEM] * 6,
        out_specs=ANY,
        scratch=[
            pltpu.VMEM((512, 1024), BF16),
            pltpu.VMEM((4096, 128), F32),
            pltpu.SemaphoreType.DMA((32,)),
        ],
    )(part, mirror.reshape(8, 16, 32, 128), gather, virb, vira, occ_lanes)
    return result.reshape(16, 256, 128)


def solution(mesh):
    fine = Mesh(mesh.devices.reshape(4, 2, 2, 4, 2), ALL)
    placed = (P(OJ, OI, None), P(OJ, OI, None), P(ALL, None), P(), P())
    return jax.shard_map(
        local, mesh=fine, in_specs=placed, out_specs=P(OJ, None, OI), check_vma=False
    )
```

time: 1030 us -> 115 us (0.11)
  waiting for transfers between devices: 861 us -> 0.93 us
  local copies, waits for them, and re-layouts: 90 us -> 0.94 us
  blocking collectives: 32.5 us -> 90.8 us
  matrix products: 19.1 us -> 0 us
  Pallas kernels: 0 us -> 16.2 us
  between operations: 13.5 us -> 0.11 us
    reduce_scatter x1 -> x0, waiting for transfers between devices: 647 us -> none  [local(): lax.psum_scatter(all_terms, ('oi', 'oj'), scatter_dimension=0, tiled=True)]
    all_gather x1 -> x0, waiting for transfers between devices: 196 us -> none  [local(): hole_ints = lax.all_gather(hole_part, ('oi', 'oj'), axis=0, tiled=True)]
    all_to_all x2 -> x4, blocking collectives: 32.5 us -> 90.8 us  [the longest x1 28 us: local(): lax.all_to_all(half_part.reshape(64, 8, 1024), CHIPS, 0, 0, tiled=False)]
    unnamed x14 -> x8, local copies, waits for them, and re-layouts: 22.5 us -> 0.01 us
    reshape x7 -> x1, local copies, waits for them, and re-layouts: 20.4 us -> 0.83 us  [local(): fac = hole_factors.reshape(256, 32)]
    all_to_all x5 -> x0, local copies, waits for them, and re-layouts: 18.9 us -> none  [the longest x3 7.14 us: local(): lax.all_to_all(blocks, 'oi', split_axis=3, concat_axis=2, tiled=True)]
    all_to_all x1 -> x0, waiting for transfers between devices: 16.9 us -> none  [local(): lax.all_to_all(lax.all_to_all(blocks, 'oi', split_axis=3, concat_axis=2,...]
    dot_general x3 -> x0, matrix products: 16.6 us -> none  [the longest x1 8.27 us: local(): jnp.einsum('prk,prl->rkl', left_rows, right_rows)]
  transfers between devices with their start and end apart: 3 -> 4, of which waited for: 3 -> 2; matrix products, arithmetic and copies ran while one was open for 0% -> 1% of each run, Pallas kernels for 0% -> 6%
where the time goes in v2:
time: 115 us; the launch traced here: 114 us
  blocking collectives  90.8 us (79%)
  Pallas kernels  16.2 us (14%)
  starting transfers between devices  5.29 us (5%)
    all_to_all x1, blocking collectives, local(): lax.all_to_all(half_part.reshape(64, 8, 1024), CHIPS, 0, 0, tiled=False)  28 us
    all_to_all x1, blocking collectives, local(): lax.all_to_all(outgoing.reshape(128, 32, 128), ALL, 0, 0, tiled=False)  24 us
    all_to_all x1, blocking collectives, local(): hole_own = lax.all_to_all(sent, CHIPS, 0, 0, tiled=False).reshape(512, 1024)  21.5 us
    all_to_all x1, blocking collectives, local(): part = lax.all_to_all(chunks, OI, 0, 0, tiled=False)  17.3 us
    pallas_call x1, Pallas kernels, local(): call(final_kernel, 'final', shape((4096, 128), F32), [VMEM] * 6, out_spec...  4.07 us
    ppermute x1, starting transfers between devices, local(): hole_peer = lax.ppermute(hole_own, 'c', SWAP)  3.2 us
    pallas_call x1, Pallas kernels, local(): call(own_kernel, 'own', square, [SMEM] + [VMEM] * 4, scratch=pieces + [pl...  2.71 us
  transfers between devices with their start and end apart: 4, of which 2 were waited for; matrix products, arithmetic and copies ran while one was open for 1% of the time, Pallas kernels for 6%

profile of v2, /device:TPU:1, one launch (start us, length us, event | category | flops | bytes accessed | tf_op | source)
XLA Modules:
  0.0 114.3 jit_solution(13357169258685195224)
XLA Ops:
  0.0 0.0 copy-start
  0.0 0.0 copy-start.1
  0.0 1.4 %collective-permute-start.1 = (bf16[512,1024]{1,0:T(8,128)(2,1)}, bf16[512,1024]{1,0:T(8,128)(2,1)S(1)}, u32[]{:S(2)}, u32[]{:S(2)}) collective-permute-start(bf16[512,1024]{1,0:T(8,128)(2,1)} %bitcast.11), channel_id=1, source_target_pairs={{0,1},{1,0},{2,3},{3,2},{4,5},{5,4},{6,7},{7,6},{8,9},{9,8},{10,11... | collective-permute-start | bytes 3145736 | tf_op jit(solution)/shard_map/ppermute | solution.py:199
  1.4 0.0 collective-permute-start.2
  1.4 0.8 reshape.35.fac
  2.2 0.7 collective-permute-start
  2.9 1.9 %density.1.start = f32[512,1024]{1,0:T(8,128)S(1)} custom-call(s32[1]{0:T(128)} %bitcast.core.half, bf16[256,32]{1,0:T(8,128)(2,1)S(1)} %reshape.35.fac), custom_call_target="tpu_custom_call" | custom-call | tf_op jit(solution)/shard_map/density/pallas_call | solution.py:203
  4.9 0.7 collective-permute-done.fac
  5.5 0.0 copy-done
  5.5 0.0 copy-done.1
  5.5 2.7 %own.1.start = f32[512,1024]{1,0:T(8,128)S(1)} custom-call(s32[1]{0:T(128)} %bitcast.core.half, f32[512,1024]{1,0:T(8,128)S(1)} %density.1.start, bf16[256,32]{1,0:T(8,128)(2,1)S(1)} %collective-permute-done.fac, bf16[512,1024]{1,0:T(8,128)(2,1)S(1)} %bitcast.12, bf16[512,1024]{1,0:T(8,128)(2,1)S(1)} %bitcast.16), custom_call_target="tpu_custom_call" | custom-call | tf_op jit(solution)/shard_map/own/pallas_call | solution.py:204
  8.2 0.0 collective-permute-done.1.amp
  8.3 0.0 collective-permute-done.2.ints
  8.3 2.1 %peer.1 = bf16[512,1024]{1,0:T(8,128)(2,1)S(1)} custom-call(s32[1]{0:T(128)} %bitcast.core.half, f32[512,1024]{1,0:T(8,128)S(1)} %own.1.start, bf16[512,1024]{1,0:T(8,128)(2,1)S(1)} %collective-permute-done.1.amp, bf16[512,1024]{1,0:T(8,128)(2,1)} %collective-permute-done.2.ints), custom_call_target="tpu_custom_call" | custom-call | tf_op jit(solution)/shard_map/peer/pallas_call | solution.py:207
  10.3 28.0 %all_to_all.20.parts = bf16[64,8,1024]{2,1,0:T(8,128)(2,1)S(1)} all-to-all(bf16[64,8,1024]{2,1,0:T(8,128)(2,1)S(1)} %bitcast.23), channel_id=1, replica_groups=mesh['x'=4,'zl'=2,'zh'=2,'y'=4,'c'=2] {'x','y','zh','zl'}, dimensions={0} | all-to-all | bytes 2097152 | tf_op jit(solution)/shard_map/all_to_all | solution.py:210
  38.3 0.0 copy-start.3
  38.3 0.2 sum.1
  38.5 21.5 %all_to_all.21 = bf16[64,8,1024]{2,1,0:T(8,128)(2,1)S(1)} all-to-all(bf16[64,8,1024]{2,1,0:T(8,128)(2,1)S(1)} %sum.1), channel_id=1, replica_groups=mesh['x'=4,'zl'=2,'zh'=2,'y'=4,'c'=2] {'x','y','zh','zl'}, dimensions={0} | all-to-all | bytes 2097152 | tf_op jit(solution)/shard_map/all_to_all | solution.py:212
  60.1 3.2 %collective-permute-start.3 = (bf16[512,1024]{1,0:T(8,128)(2,1)S(1)}, bf16[512,1024]{1,0:T(8,128)(2,1)}, u32[]{:S(2)}, u32[]{:S(2)}) collective-permute-start(bf16[512,1024]{1,0:T(8,128)(2,1)S(1)} %bitcast.20), channel_id=1, source_target_pairs={{0,1},{1,0},{2,3},{3,2},{4,5},{5,4},{6,7},{7,6},{8,9},{9,8},{10,11... | collective-permute-start | bytes 3145736 | tf_op jit(solution)/shard_map/ppermute | solution.py:213
  63.3 0.0 copy-done.3
  63.3 0.1 broadcast_in_dim.14
  63.3 0.1 pad_add_fusion.place
  63.4 0.0 copy-start.2
  63.4 0.7 ladder_own.1.refs_0_
  64.2 0.0 copy-done.2
  64.2 1.2 %tables.1 = (bf16[1024,1024]{1,0:T(8,128)(2,1)S(1)}, bf16[1024,1024]{1,0:T(8,128)(2,1)S(1)}, f32[256,128]{1,0:T(8,128)S(1)}, f32[16,128]{1,0:T(8,128)S(1)}, f32[16,128]{1,0:T(8,128)S(1)}) custom-call(s32[2]{0:T(128)S(1)} %pad_add_fusion.place, f32[8,256]{1,0:T(8,128)S(1)} %broadcast_in_dim.6.vir, f32[8,128]{1,0:T(8,128)S(1)} %broadcast_in_dim.15.occ), custom_call_target="tpu_custom_call" | custom-call | tf_op jit(solution)/shard_map/tables/pallas_call | solution.py:220
  65.4 0.3 collective-permute-done.3.hole
  65.7 2.0 %ladder_peer.1 = bf16[8,512,128]{2,1,0:T(8,128)(2,1)S(1)} custom-call(s32[1]{0:T(128)S(6)} %sub.3.half, bf16[512,1024]{1,0:T(8,128)(2,1)S(1)} %bitcast.14, bf16[512,1024]{1,0:T(8,128)(2,1)} %collective-permute-done.3.hole, bf16[512,1024]{1,0:T(8,128)(2,1)S(1)} %bitcast.18, bf16[8,512,128]{2,1,0:T(8,128)(2,1)S(1)} %ladder_own.1.refs_0_), custom_call_target="tpu_custom_call", output_to_operand_aliasing={{}: (4, {})} | custom-call | tf_op jit(solution)/shard_map/ladder_peer/pallas_call | solution.py:233
  67.6 17.3 %all_to_all.22.part = bf16[8,512,128]{2,1,0:T(8,128)(2,1)S(1)} all-to-all(bf16[8,512,128]{2,1,0:T(8,128)(2,1)S(1)} %ladder_peer.1), channel_id=1, replica_groups=mesh['x'=4,'zl'=2,'zh'=2,'y'=4,'c'=2] {'x','zl'}, dimensions={0} | all-to-all | bytes 2097152 | tf_op jit(solution)/shard_map/all_to_all | solution.py:236
  84.9 1.3 %spread.1 = bf16[8,16,32,128]{3,2,1,0:T(8,128)(2,1)S(1)} custom-call(bf16[8,16,32,128]{3,2,1,0:T(8,128)(2,1)S(1)} %bitcast.19, bf16[1024,1024]{1,0:T(8,128)(2,1)S(1)} %get-tuple-element.24.perm), custom_call_target="tpu_custom_call" | custom-call | tf_op jit(solution)/shard_map/spread/pallas_call | solution.py:237
  86.2 24.0 %all_to_all.23 = bf16[128,32,128]{2,1,0:T(8,128)(2,1)S(1)} all-to-all(bf16[128,32,128]{2,1,0:T(8,128)(2,1)S(1)} %bitcast.24), channel_id=1, replica_groups=mesh['x'=4,'zl'=2,'zh'=2,'y'=4,'c'=2] {'x','zl','zh','y','c'}, dimensions={0} | all-to-all | bytes 2097152 | tf_op jit(solution)/shard_map/all_to_all | solution.py:244
  110.2 4.1 %final.1 = f32[4096,128]{1,0:T(8,128)} custom-call(bf16[8,512,128]{2,1,0:T(8,128)(2,1)S(1)} %all_to_all.22.part, bf16[8,16,32,128]{3,2,1,0:T(8,128)(2,1)S(1)} %bitcast.22, bf16[1024,1024]{1,0:T(8,128)(2,1)S(1)} %get-tuple-element.25.perm, f32[256,128]{1,0:T(8,128)S(1)} %get-tuple-element.26.virb, f32[16,128]{1,0:T(8,128)S(1)} %get-tuple-element.27.vira, ...), custom_call_target="tpu_custom_call" | custom-call | tf_op jit(solution)/shard_map/final/pallas_call | solution.py:245
  (3 shorter events, 0.0 us)
Async XLA Ops:
  0.0 5.5 %copy-start = (bf16[16,32,1024]{2,1,0:T(8,128)(2,1)S(1)}, bf16[16,32,1024]{2,1,0:T(8,128)(2,1)}, u32[]{:S(2)}) copy-start(bf16[16,32,1024]{2,1,0:T(8,128)(2,1)} %param.5) | copy-start | bytes 3145732
  0.0 5.5 %copy-start.1 = (bf16[16,32,1024]{2,1,0:T(8,128)(2,1)S(1)}, bf16[16,32,1024]{2,1,0:T(8,128)(2,1)}, u32[]{:S(2)}) copy-start(bf16[16,32,1024]{2,1,0:T(8,128)(2,1)} %param.6) | copy-start | bytes 3145732
  0.0 8.2 %collective-permute-start.1 = (bf16[512,1024]{1,0:T(8,128)(2,1)}, bf16[512,1024]{1,0:T(8,128)(2,1)S(1)}, u32[]{:S(2)}, u32[]{:S(2)}) collective-permute-start(bf16[512,1024]{1,0:T(8,128)(2,1)} %bitcast.11), channel_id=1, source_target_pairs={{0,1},{1,0},{2,3},{3,2},{4,5},{5,4},{6,7},{7,6},{8,9},{9,8},{10,11... | collective-permute-start | bytes 3145736 | tf_op jit(solution)/shard_map/ppermute | solution.py:199
  1.4 6.9 %collective-permute-start.2 = (bf16[512,1024]{1,0:T(8,128)(2,1)}, bf16[512,1024]{1,0:T(8,128)(2,1)}, u32[]{:S(2)}, u32[]{:S(2)}) collective-permute-start(bf16[512,1024]{1,0:T(8,128)(2,1)} %bitcast.15), channel_id=1, source_target_pairs={{0,1},{1,0},{2,3},{3,2},{4,5},{5,4},{6,7},{7,6},{8,9},{9,8},{10,11... | collective-permute-start | bytes 3145736 | tf_op jit(solution)/shard_map/ppermute | solution.py:200
  2.2 3.3 %collective-permute-start = (bf16[256,32]{1,0:T(8,128)(2,1)S(1)}, bf16[256,32]{1,0:T(8,128)(2,1)S(1)}, u32[]{:S(2)}, u32[]{:S(2)}) collective-permute-start(bf16[256,32]{1,0:T(8,128)(2,1)S(1)} %reshape.35.fac), channel_id=1, source_target_pairs={{0,1},{1,0},{2,3},{3,2},{4,5},{5,4},{6,7},{7,6},{8,9},{9,8},{10,11... | collective-permute-start | bytes 49160 | tf_op jit(solution)/shard_map/ppermute | solution.py:198
  38.3 25.0 %copy-start.3 = (f32[32]{0:T(128)S(1)}, f32[32]{0:T(128)}, u32[]{:S(2)}) copy-start(f32[32]{0:T(128)} %param.8) | copy-start | bytes 388
  60.1 5.6 %collective-permute-start.3 = (bf16[512,1024]{1,0:T(8,128)(2,1)S(1)}, bf16[512,1024]{1,0:T(8,128)(2,1)}, u32[]{:S(2)}, u32[]{:S(2)}) collective-permute-start(bf16[512,1024]{1,0:T(8,128)(2,1)S(1)} %bitcast.20), channel_id=1, source_target_pairs={{0,1},{1,0},{2,3},{3,2},{4,5},{5,4},{6,7},{7,6},{8,9},{9,8},{10,11... | collective-permute-start | bytes 3145736 | tf_op jit(solution)/shard_map/ppermute | solution.py:213
  63.4 0.8 copy-start.2

commit v3 on v2

--- a/solution.py
+++ b/solution.py
@@ -33,7 +33,7 @@
     return jax.ShapeDtypeStruct(dims, dtype)
 
 
-def tables_kernel(place, vir, occ, spread, gather, virb, vira, occ_lanes):
+def tables_kernel(after, spread, gather):
     row = lax.broadcasted_iota(jnp.int32, (128, 128), 0)
     lane = lax.broadcasted_iota(jnp.int32, (128, 128), 1)
 
@@ -52,16 +52,24 @@
             cols = slice(b * 128, b * 128 + 128)
             spread[rows, cols] = out_rows[b] * out_lanes
             gather[rows, cols] = in_rows[b] * in_lanes
+
+
+def energies(first_tile, rows_tile, both, virb, vira, occ_lanes):
+    row = lax.broadcasted_iota(jnp.int32, (128, 128), 0)
+    lane = lax.broadcasted_iota(jnp.int32, (128, 128), 1)
     for half in range(2):
         cols = slice(half * 128, half * 128 + 128)
-        diagonal = jnp.where(row == lane, jnp.broadcast_to(vir[:1, cols], (128, 128)), 0.0)
+        wide = jnp.broadcast_to(both[:1, cols], (128, 128))
+        diagonal = jnp.where(row == lane, wide, 0.0)
         virb[cols, :] = jnp.broadcast_to(jnp.sum(diagonal, axis=1, keepdims=True), (128, 128))
-    vira[...] = virb[pl.ds(pl.multiple_of(place[1] * 16, 16), 16), :]
-    second = occ[...]
+    vira[...] = virb[pl.ds(pl.multiple_of(rows_tile[0] * 16, 16), 16), :]
     one = lane[:8]
+    second = both[:, 256:]
+    second = second + pltpu.roll(second, 32, 1)
+    second = second + pltpu.roll(second, 64, 1)
     first = jnp.zeros((8, 128), F32)
     for i in range(4):
-        mine = jnp.where(one == place[0] * 4 + i, second, 0.0)
+        mine = jnp.where(one == first_tile[0] * 4 + i, second, 0.0)
         value = jnp.broadcast_to(jnp.sum(mine, axis=1, keepdims=True), (8, 128))
         first = jnp.where(one // 32 == i, value, first)
     occ_lanes[:8] = first
@@ -150,48 +158,42 @@
 
 
 def final_kernel(part, mirror, perm, virb, vira, occ_lanes, out, wide, held, sems):
+    for q in range(8):
+        wide[:, q * 128 : q * 128 + 128] = mirror[q].reshape(512, 128)
+    for al in range(0, 8, 2):
+        moved = jnp.dot(
+            wide[...], perm[:, al * 128 : al * 128 + 256], preferred_element_type=F32
+        )
+        for o in range(16):
+            for ah in range(2):
+                base = (o * 2 + ah) * 16
+                for s in range(2):
+                    held[pl.ds(o * 16 + ah * 8 + al + s, 16, stride=256), :] = moved[
+                        base : base + 16, s * 128 : s * 128 + 128
+                    ]
     first, second = occ_lanes[:1], occ_lanes[8:9]
 
-    def copy(a, half):
-        rows = pl.ds(pl.multiple_of(a * 256 + half * 128, 128), 128)
-        return pltpu.make_async_copy(held.at[rows], out.at[rows], sems.at[half * 16 + a])
-
-    for half in range(2):
-        mine = slice(half * 256, half * 256 + 256)
-        for q in range(8):
-            wide[mine, q * 128 : q * 128 + 128] = mirror[q, half * 8 : half * 8 + 8].reshape(256, 128)
-        for al in range(0, 8, 2):
-            moved = jnp.dot(
-                wide[mine, :], perm[:, al * 128 : al * 128 + 256], preferred_element_type=F32
-            )
-            for o in range(8):
-                for ah in range(2):
-                    base = (o * 2 + ah) * 16
-                    for s in range(2):
-                        row = (half * 8 + o) * 16 + ah * 8 + al + s
-                        held[pl.ds(row, 16, stride=256), :] = moved[
-                            base : base + 16, s * 128 : s * 128 + 128
-                        ]
-
-        def one(a, carry):
-            energy = vira[pl.ds(a, 1), :]
-            for r in range(half * 4, half * 4 + 4):
-                rows = pl.ds(pl.multiple_of(a * 256 + r * 32, 32), 32)
-                direct = part[r, pl.ds(pl.multiple_of(a * 32, 32), 32), :].astype(F32)
-                low = energy + virb[r * 32 : r * 32 + 32, :] - first - second
-                held[rows, :] = (direct + held[rows, :]) / low
-            copy(a, half).start()
-            return carry
-
-        lax.fori_loop(0, 16, one, 0)
-    for half in range(2):
-        for a in range(16):
-            copy(a, half).wait()
+    def one(a, carry):
+        energy = vira[pl.ds(a, 1), :]
+        for r in range(8):
+            rows = pl.ds(pl.multiple_of(a * 256 + r * 32, 32), 32)
+            direct = part[r, pl.ds(pl.multiple_of(a * 32, 32), 32), :].astype(F32)
+            low = energy + virb[r * 32 : r * 32 + 32, :] - first - second
+            held[rows, :] = (direct + held[rows, :]) / low
+        return carry
+
+    copies = []
+    for n in range(4):
+        lax.fori_loop(n * 4, n * 4 + 4, one, 0)
+        rows = slice(n * 1024, n * 1024 + 1024)
+        copies.append(pltpu.make_async_copy(held.at[rows], out.at[rows], sems.at[n]))
+        copies[-1].start()
+    for copy in copies:
+        copy.wait()
 
 
 def local(amplitudes, exchange_ints, hole_factors, occ_energy, vir_energy):
     core = lax.axis_index("c").astype(jnp.int32).reshape(1)
-    place = jnp.stack([lax.axis_index(OI), lax.axis_index(OJ)]).astype(jnp.int32)
     amp = amplitudes.reshape(512, 1024)
     ints = exchange_ints.reshape(512, 1024)
     fac = hole_factors.reshape(256, 32)
@@ -200,10 +202,24 @@
     ints_peer = lax.ppermute(ints, "c", SWAP)
     pieces = [pltpu.VMEM((256, 1024), F32)] * 2
     square = shape((512, 1024), F32)
-    density = call(density_kernel, "density", square, [SMEM, VMEM], scratch=pieces)(core, fac)
-    own = call(own_kernel, "own", square, [SMEM] + [VMEM] * 4, scratch=pieces + [pltpu.VMEM((512, 1024), F32)])(
-        core, density, fac_peer, amp, ints
-    )
+    both = jnp.concatenate([vir_energy, occ_energy, jnp.zeros((96,), F32)])
+    both = jnp.broadcast_to(both[None], (8, 384))
+    tiles = [lax.axis_index(a).astype(jnp.int32).reshape(1) for a in (OI, OJ)]
+    levels = call(
+        energies,
+        "energies",
+        (shape((256, 128), F32), shape((16, 128), F32), shape((16, 128), F32)),
+        [SMEM] * 2 + [VMEM],
+    )(*tiles, both)
+    fac_here, virb, vira, occ_lanes = lax.optimization_barrier((fac, *levels))
+    density = call(density_kernel, "density", square, [SMEM, VMEM], scratch=pieces)(core, fac_here)
+    own = call(
+        own_kernel,
+        "own",
+        square,
+        [SMEM] + [VMEM] * 4,
+        scratch=pieces + [pltpu.VMEM((512, 1024), F32)],
+    )(core, density, fac_peer, amp, ints)
     half_part = call(peer_kernel, "peer", shape((512, 1024)), [SMEM] + [VMEM] * 3)(
         core, own, amp_peer, ints_peer
     )
@@ -214,22 +230,9 @@
     chunks = call(ladder_kernel, "ladder_own", shape((8, 512, 128)), [SMEM] + [VMEM] * 3)(
         core, amp, hole_own, ints
     )
-    vir_row = jnp.broadcast_to(vir_energy[None], (8, 256))
-    occ_row = jnp.broadcast_to(jnp.tile(occ_energy, 4)[None], (8, 128))
-    place, hole_own = lax.optimization_barrier((place, hole_own))
-    tables = call(
-        tables_kernel,
-        "tables",
-        (
-            shape((1024, 1024)),
-            shape((1024, 1024)),
-            shape((256, 128), F32),
-            shape((16, 128), F32),
-            shape((16, 128), F32),
-        ),
-        [SMEM, VMEM, VMEM],
-    )(place, vir_row, occ_row)
-    chunks, spread, gather, virb, vira, occ_lanes = lax.optimization_barrier((chunks, *tables))
+    after, hole_own = lax.optimization_barrier((core, hole_own))
+    tables = call(tables_kernel, "tables", (shape((1024, 1024)), shape((1024, 1024))), [SMEM])(after)
+    chunks, spread, gather = lax.optimization_barrier((chunks, *tables))
     chunks = call(
         ladder_kernel, "ladder_peer", shape((8, 512, 128)), [SMEM] + [VMEM] * 4, alias={4: 0}
     )(1 - core, amp, hole_peer, ints, chunks)
@@ -251,7 +254,7 @@
         scratch=[
             pltpu.VMEM((512, 1024), BF16),
             pltpu.VMEM((4096, 128), F32),
-            pltpu.SemaphoreType.DMA((32,)),
+            pltpu.SemaphoreType.DMA((4,)),
         ],
     )(part, mirror.reshape(8, 16, 32, 128), gather, virb, vira, occ_lanes)
     return result.reshape(16, 256, 128)

time: 115 us -> 114 us (level)
  Pallas kernels: 16.2 us -> 14.4 us
    pallas_call x1, Pallas kernels: 1.97 us -> 0.74 us  [local(): call(ladder_kernel, 'ladder_peer', shape((8, 512, 128)), [SMEM] + [VMEM]...]
  transfers between devices with their start and end apart: 4 -> 4, of which waited for: 2 -> 1; matrix products, arithmetic and copies ran while one was open for 1% -> 1% of each run, Pallas kernels for 6% -> 5%
where the time goes in v3:
time: 114 us
  blocking collectives  91.5 us (80%)
  Pallas kernels  14.4 us (13%)
  starting transfers between devices  5.18 us (5%)
    all_to_all x1, blocking collectives, local(): lax.all_to_all(half_part.reshape(64, 8, 1024), CHIPS, 0, 0, tiled=False)  28.4 us
    all_to_all x1, blocking collectives, local(): lax.all_to_all(outgoing.reshape(128, 32, 128), ALL, 0, 0, tiled=False)  24.2 us
    all_to_all x1, blocking collectives, local(): hole_own = lax.all_to_all(sent, CHIPS, 0, 0, tiled=False).reshape(512, 1024)  21.5 us
    all_to_all x1, blocking collectives, local(): part = lax.all_to_all(chunks, OI, 0, 0, tiled=False)  17.3 us
    pallas_call x1, Pallas kernels, local(): call(final_kernel, 'final', shape((4096, 128), F32), [VMEM] * 6, out_spec...  3.86 us
    ppermute x1, starting transfers between devices, local(): hole_peer = lax.ppermute(hole_own, 'c', SWAP)  3.1 us
    pallas_call x1, Pallas kernels, local(): call(own_kernel, 'own', square, [SMEM] + [VMEM] * 4, scratch=pieces + [pl...  2.71 us
  transfers between devices with their start and end apart: 4, of which 1 were waited for; matrix products, arithmetic and copies ran while one was open for 1% of the time, Pallas kernels for 5%

profile of v3, /device:TPU:1, one launch (start us, length us, event | category | flops | bytes accessed | tf_op | source)
XLA Modules:
  0.0 113.7 jit_solution(8684297930279616354)
XLA Ops:
  0.0 0.0 copy-start
  0.0 0.0 copy-start.1
  0.0 1.4 %collective-permute-start.1 = (bf16[512,1024]{1,0:T(8,128)(2,1)}, bf16[512,1024]{1,0:T(8,128)(2,1)S(1)}, u32[]{:S(2)}, u32[]{:S(2)}) collective-permute-start(bf16[512,1024]{1,0:T(8,128)(2,1)} %bitcast.11), channel_id=1, source_target_pairs={{0,1},{1,0},{2,3},{3,2},{4,5},{5,4},{6,7},{7,6},{8,9},{9,8},{10,11... | collective-permute-start | bytes 3145736 | tf_op jit(solution)/shard_map/ppermute | solution.py:201
  1.4 0.0 collective-permute-start.2
  1.4 0.8 reshape.39.fac
  2.2 0.7 collective-permute-start
  2.9 0.8 pad_maximum_fusion
  3.7 0.2 energies.1
  3.9 1.9 %density.1.start = f32[512,1024]{1,0:T(8,128)S(1)} custom-call(s32[1]{0:T(128)} %bitcast.core.half.after, bf16[256,32]{1,0:T(8,128)(2,1)S(1)} %reshape.39.fac), custom_call_target="tpu_custom_call" | custom-call | tf_op jit(solution)/shard_map/density/pallas_call | solution.py:215
  5.9 0.0 collective-permute-done.fac
  5.9 0.0 copy-done
  5.9 0.0 copy-done.1
  5.9 2.7 %own.1.start = f32[512,1024]{1,0:T(8,128)S(1)} custom-call(s32[1]{0:T(128)} %bitcast.core.half.after, f32[512,1024]{1,0:T(8,128)S(1)} %density.1.start, bf16[256,32]{1,0:T(8,128)(2,1)S(1)} %collective-permute-done.fac, bf16[512,1024]{1,0:T(8,128)(2,1)S(1)} %bitcast.12, bf16[512,1024]{1,0:T(8,128)(2,1)S(1)} %bitcast.16), custom_call_target="tpu_custom_call" | custom-call | tf_op jit(solution)/shard_map/own/pallas_call | solution.py:216
  8.6 0.0 collective-permute-done.1.amp
  8.6 0.0 collective-permute-done.2.ints
  8.6 2.0 %peer.1 = bf16[512,1024]{1,0:T(8,128)(2,1)S(1)} custom-call(s32[1]{0:T(128)} %bitcast.core.half.after, f32[512,1024]{1,0:T(8,128)S(1)} %own.1.start, bf16[512,1024]{1,0:T(8,128)(2,1)S(1)} %collective-permute-done.1.amp, bf16[512,1024]{1,0:T(8,128)(2,1)} %collective-permute-done.2.ints), custom_call_target="tpu_custom_call" | custom-call | tf_op jit(solution)/shard_map/peer/pallas_call | solution.py:223
  10.7 28.4 %all_to_all.20.parts = bf16[64,8,1024]{2,1,0:T(8,128)(2,1)S(1)} all-to-all(bf16[64,8,1024]{2,1,0:T(8,128)(2,1)S(1)} %bitcast.23), channel_id=1, replica_groups=mesh['x'=4,'zl'=2,'zh'=2,'y'=4,'c'=2] {'x','y','zh','zl'}, dimensions={0} | all-to-all | bytes 2097152 | tf_op jit(solution)/shard_map/all_to_all | solution.py:226
  39.1 0.2 sum.1
  39.3 21.5 %all_to_all.21 = bf16[64,8,1024]{2,1,0:T(8,128)(2,1)S(1)} all-to-all(bf16[64,8,1024]{2,1,0:T(8,128)(2,1)S(1)} %sum.1), channel_id=1, replica_groups=mesh['x'=4,'zl'=2,'zh'=2,'y'=4,'c'=2] {'x','y','zh','zl'}, dimensions={0} | all-to-all | bytes 2097152 | tf_op jit(solution)/shard_map/all_to_all | solution.py:228
  60.9 3.1 %collective-permute-start.3 = (bf16[512,1024]{1,0:T(8,128)(2,1)S(1)}, bf16[512,1024]{1,0:T(8,128)(2,1)S(1)}, u32[]{:S(2)}, u32[]{:S(2)}) collective-permute-start(bf16[512,1024]{1,0:T(8,128)(2,1)S(1)} %bitcast.20), channel_id=1, source_target_pairs={{0,1},{1,0},{2,3},{3,2},{4,5},{5,4},{6,7},{7,6},{8,9},{9,8},{10,11... | collective-permute-start | bytes 3145736 | tf_op jit(solution)/shard_map/ppermute | solution.py:229
  64.0 0.7 ladder_own.1.refs_0_
  64.7 0.7 tables.1
  65.4 0.9 collective-permute-done.3.hole
  66.2 0.7 ladder_peer.1
  67.0 17.3 %all_to_all.22.part = bf16[8,512,128]{2,1,0:T(8,128)(2,1)S(1)} all-to-all(bf16[8,512,128]{2,1,0:T(8,128)(2,1)S(1)} %ladder_peer.1), channel_id=1, replica_groups=mesh['x'=4,'zl'=2,'zh'=2,'y'=4,'c'=2] {'x','zl'}, dimensions={0} | all-to-all | bytes 2097152 | tf_op jit(solution)/shard_map/all_to_all | solution.py:239
  84.3 1.3 %spread.1 = bf16[8,16,32,128]{3,2,1,0:T(8,128)(2,1)S(1)} custom-call(bf16[8,16,32,128]{3,2,1,0:T(8,128)(2,1)S(1)} %bitcast.19, bf16[1024,1024]{1,0:T(8,128)(2,1)S(1)} %get-tuple-element.26.perm), custom_call_target="tpu_custom_call" | custom-call | tf_op jit(solution)/shard_map/spread/pallas_call | solution.py:240
  85.6 24.2 %all_to_all.23 = bf16[128,32,128]{2,1,0:T(8,128)(2,1)S(1)} all-to-all(bf16[128,32,128]{2,1,0:T(8,128)(2,1)S(1)} %bitcast.24), channel_id=1, replica_groups=mesh['x'=4,'zl'=2,'zh'=2,'y'=4,'c'=2] {'x','zl','zh','y','c'}, dimensions={0} | all-to-all | bytes 2097152 | tf_op jit(solution)/shard_map/all_to_all | solution.py:247
  109.8 3.9 %final.1 = f32[4096,128]{1,0:T(8,128)} custom-call(bf16[8,512,128]{2,1,0:T(8,128)(2,1)S(1)} %all_to_all.22.part, bf16[8,16,32,128]{3,2,1,0:T(8,128)(2,1)S(1)} %bitcast.22, bf16[1024,1024]{1,0:T(8,128)(2,1)S(1)} %get-tuple-element.27.perm, f32[256,128]{1,0:T(8,128)S(1)} %get-tuple-element.28.virb, f32[16,128]{1,0:T(8,128)S(1)} %get-tuple-element.29.vira, ...), custom_call_target="tpu_custom_call" | custom-call | tf_op jit(solution)/shard_map/final/pallas_call | solution.py:248
  (2 shorter events, 0.0 us)
Async XLA Ops:
  0.0 5.9 %copy-start = (bf16[16,32,1024]{2,1,0:T(8,128)(2,1)S(1)}, bf16[16,32,1024]{2,1,0:T(8,128)(2,1)}, u32[]{:S(2)}) copy-start(bf16[16,32,1024]{2,1,0:T(8,128)(2,1)} %param.5) | copy-start | bytes 3145732
  0.0 5.9 %copy-start.1 = (bf16[16,32,1024]{2,1,0:T(8,128)(2,1)S(1)}, bf16[16,32,1024]{2,1,0:T(8,128)(2,1)}, u32[]{:S(2)}) copy-start(bf16[16,32,1024]{2,1,0:T(8,128)(2,1)} %param.6) | copy-start | bytes 3145732
  0.0 8.6 %collective-permute-start.1 = (bf16[512,1024]{1,0:T(8,128)(2,1)}, bf16[512,1024]{1,0:T(8,128)(2,1)S(1)}, u32[]{:S(2)}, u32[]{:S(2)}) collective-permute-start(bf16[512,1024]{1,0:T(8,128)(2,1)} %bitcast.11), channel_id=1, source_target_pairs={{0,1},{1,0},{2,3},{3,2},{4,5},{5,4},{6,7},{7,6},{8,9},{9,8},{10,11... | collective-permute-start | bytes 3145736 | tf_op jit(solution)/shard_map/ppermute | solution.py:201
  1.4 7.2 %collective-permute-start.2 = (bf16[512,1024]{1,0:T(8,128)(2,1)}, bf16[512,1024]{1,0:T(8,128)(2,1)}, u32[]{:S(2)}, u32[]{:S(2)}) collective-permute-start(bf16[512,1024]{1,0:T(8,128)(2,1)} %bitcast.15), channel_id=1, source_target_pairs={{0,1},{1,0},{2,3},{3,2},{4,5},{5,4},{6,7},{7,6},{8,9},{9,8},{10,11... | collective-permute-start | bytes 3145736 | tf_op jit(solution)/shard_map/ppermute | solution.py:202
  2.2 3.6 %collective-permute-start = (bf16[256,32]{1,0:T(8,128)(2,1)S(1)}, bf16[256,32]{1,0:T(8,128)(2,1)S(1)}, u32[]{:S(2)}, u32[]{:S(2)}) collective-permute-start(bf16[256,32]{1,0:T(8,128)(2,1)S(1)} %reshape.39.fac), channel_id=1, source_target_pairs={{0,1},{1,0},{2,3},{3,2},{4,5},{5,4},{6,7},{7,6},{8,9},{9,8},{10,11... | collective-permute-start | bytes 49160 | tf_op jit(solution)/shard_map/ppermute | solution.py:200
  60.9 5.4 %collective-permute-start.3 = (bf16[512,1024]{1,0:T(8,128)(2,1)S(1)}, bf16[512,1024]{1,0:T(8,128)(2,1)S(1)}, u32[]{:S(2)}, u32[]{:S(2)}) collective-permute-start(bf16[512,1024]{1,0:T(8,128)(2,1)S(1)} %bitcast.20), channel_id=1, source_target_pairs={{0,1},{1,0},{2,3},{3,2},{4,5},{5,4},{6,7},{7,6},{8,9},{9,8},{10,11... | collective-permute-start | bytes 3145736 | tf_op jit(solution)/shard_map/ppermute | solution.py:229

commit v4 on v3

--- a/solution.py
+++ b/solution.py
@@ -107,17 +107,20 @@
     add_density(core, fac, left, right, None, out)
 
 
-def own_kernel(core, start, fac, amp, ints, out, left, right, held):
+def own_kernel(core, start, amp, ints, out):
     for g in range(4):
         rows = slice(g * 128, g * 128 + 128)
-        held[rows, :] = start[rows, :] + quadratic(core, g, amp, ints)
-    add_density(core, fac, left, right, held, out)
-
-
-def peer_kernel(core, start, amp, ints, out):
+        out[rows, :] = start[rows, :] + quadratic(core, g, amp, ints)
+
+
+def peer_kernel(core, start, fac, amp, ints, out, left, right, held, here, sem):
+    copy = pltpu.make_async_copy(ints, here, sem)
+    copy.start()
+    add_density(core, fac, left, right, start, held)
+    copy.wait()
     for g in range(4):
         rows = slice(g * 128, g * 128 + 128)
-        out[rows, :] = (start[rows, :] + quadratic(core, g, amp, ints)).astype(BF16)
+        out[rows, :] = (held[rows, :] + quadratic(core, g, amp, here)).astype(BF16)
 
 
 def sum_kernel(parts, out):
@@ -213,16 +216,19 @@
     )(*tiles, both)
     fac_here, virb, vira, occ_lanes = lax.optimization_barrier((fac, *levels))
     density = call(density_kernel, "density", square, [SMEM, VMEM], scratch=pieces)(core, fac_here)
-    own = call(
-        own_kernel,
-        "own",
-        square,
-        [SMEM] + [VMEM] * 4,
-        scratch=pieces + [pltpu.VMEM((512, 1024), F32)],
-    )(core, density, fac_peer, amp, ints)
-    half_part = call(peer_kernel, "peer", shape((512, 1024)), [SMEM] + [VMEM] * 3)(
-        core, own, amp_peer, ints_peer
-    )
+    own = call(own_kernel, "own", square, [SMEM] + [VMEM] * 3)(core, density, amp, ints)
+    half_part = call(
+        peer_kernel,
+        "peer",
+        shape((512, 1024)),
+        [SMEM, VMEM, VMEM, VMEM, ANY],
+        scratch=pieces
+        + [
+            pltpu.VMEM((512, 1024), F32),
+            pltpu.VMEM((512, 1024), BF16),
+            pltpu.SemaphoreType.DMA(()),
+        ],
+    )(core, own, fac_peer, amp_peer, ints_peer)
     parts = lax.all_to_all(half_part.reshape(64, 8, 1024), CHIPS, 0, 0, tiled=False)
     sent = call(sum_kernel, "sum", shape((64, 8, 1024)), [VMEM])(parts)
     hole_own = lax.all_to_all(sent, CHIPS, 0, 0, tiled=False).reshape(512, 1024)

time: 114 us -> 113 us (level)
  transfers between devices with their start and end apart: 4 -> 4, of which waited for: 1 -> 1; matrix products, arithmetic and copies ran while one was open for 1% -> 1% of each run, Pallas kernels for 5% -> 4%
where the time goes in v4:
time: 113 us
  blocking collectives  91.4 us (81%)
  Pallas kernels  13.4 us (12%)
  starting transfers between devices  5.19 us (5%)
    all_to_all x1, blocking collectives, local(): lax.all_to_all(half_part.reshape(64, 8, 1024), CHIPS, 0, 0, tiled=False)  28.4 us
    all_to_all x1, blocking collectives, local(): lax.all_to_all(outgoing.reshape(128, 32, 128), ALL, 0, 0, tiled=False)  24.2 us
    all_to_all x1, blocking collectives, local(): hole_own = lax.all_to_all(sent, CHIPS, 0, 0, tiled=False).reshape(512, 1024)  21.5 us
    all_to_all x1, blocking collectives, local(): part = lax.all_to_all(chunks, OI, 0, 0, tiled=False)  17.3 us
    pallas_call x1, Pallas kernels, local(): call(final_kernel, 'final', shape((4096, 128), F32), [VMEM] * 6, out_spec...  3.87 us
    ppermute x1, starting transfers between devices, local(): hole_peer = lax.ppermute(hole_own, 'c', SWAP)  3.11 us
    pallas_call x1, Pallas kernels, local(): call(peer_kernel, 'peer', shape((512, 1024)), [SMEM, VMEM, VMEM, VMEM, AN...  2.83 us
  transfers between devices with their start and end apart: 4, of which 1 were waited for; matrix products, arithmetic and copies ran while one was open for 1% of the time, Pallas kernels for 4%

profile of v4, /device:TPU:1, one launch (start us, length us, event | category | flops | bytes accessed | tf_op | source)
XLA Modules:
  0.0 112.6 jit_solution(17690163023818450601)
XLA Ops:
  0.0 0.0 copy-start
  0.0 0.0 copy-start.1
  0.0 1.4 %collective-permute-start.1 = (bf16[512,1024]{1,0:T(8,128)(2,1)}, bf16[512,1024]{1,0:T(8,128)(2,1)S(1)}, u32[]{:S(2)}, u32[]{:S(2)}) collective-permute-start(bf16[512,1024]{1,0:T(8,128)(2,1)} %bitcast.11), channel_id=1, source_target_pairs={{0,1},{1,0},{2,3},{3,2},{4,5},{5,4},{6,7},{7,6},{8,9},{9,8},{10,11... | collective-permute-start | bytes 3145736 | tf_op jit(solution)/shard_map/ppermute | solution.py:204
  1.4 0.0 collective-permute-start.2
  1.4 0.8 reshape.39.fac
  2.2 0.7 collective-permute-start
  2.9 0.8 pad_maximum_fusion
  3.7 0.2 energies.1
  3.9 1.9 %density.1.start = f32[512,1024]{1,0:T(8,128)S(1)} custom-call(s32[1]{0:T(128)} %bitcast.core.half.after, bf16[256,32]{1,0:T(8,128)(2,1)S(1)} %reshape.39.fac), custom_call_target="tpu_custom_call" | custom-call | tf_op jit(solution)/shard_map/density/pallas_call | solution.py:218
  5.9 0.0 copy-done
  5.9 0.0 copy-done.1
  5.9 0.8 own.1.start
  6.7 0.0 collective-permute-done.fac
  6.7 0.0 collective-permute-done.1.amp
  6.7 0.0 collective-permute-done.2.ints
  6.8 2.8 %peer.1 = bf16[512,1024]{1,0:T(8,128)(2,1)S(1)} custom-call(s32[1]{0:T(128)} %bitcast.core.half.after, f32[512,1024]{1,0:T(8,128)S(1)} %own.1.start, bf16[256,32]{1,0:T(8,128)(2,1)S(1)} %collective-permute-done.fac, bf16[512,1024]{1,0:T(8,128)(2,1)S(1)} %collective-permute-done.1.amp, bf16[512,1024]{1,0:T(8,128)(2,1)} %collective-permute-done.2.ints), custom_call_target="tpu_custom_call" | custom-call | tf_op jit(solution)/shard_map/peer/pallas_call | solution.py:220
  9.6 28.4 %all_to_all.20.parts = bf16[64,8,1024]{2,1,0:T(8,128)(2,1)S(1)} all-to-all(bf16[64,8,1024]{2,1,0:T(8,128)(2,1)S(1)} %bitcast.23), channel_id=1, replica_groups=mesh['x'=4,'zl'=2,'zh'=2,'y'=4,'c'=2] {'x','y','zh','zl'}, dimensions={0} | all-to-all | bytes 2097152 | tf_op jit(solution)/shard_map/all_to_all | solution.py:232
  38.0 0.2 sum.1
  38.2 21.5 %all_to_all.21 = bf16[64,8,1024]{2,1,0:T(8,128)(2,1)S(1)} all-to-all(bf16[64,8,1024]{2,1,0:T(8,128)(2,1)S(1)} %sum.1), channel_id=1, replica_groups=mesh['x'=4,'zl'=2,'zh'=2,'y'=4,'c'=2] {'x','y','zh','zl'}, dimensions={0} | all-to-all | bytes 2097152 | tf_op jit(solution)/shard_map/all_to_all | solution.py:234
  59.7 3.1 %collective-permute-start.3 = (bf16[512,1024]{1,0:T(8,128)(2,1)S(1)}, bf16[512,1024]{1,0:T(8,128)(2,1)S(1)}, u32[]{:S(2)}, u32[]{:S(2)}) collective-permute-start(bf16[512,1024]{1,0:T(8,128)(2,1)S(1)} %bitcast.20), channel_id=1, source_target_pairs={{0,1},{1,0},{2,3},{3,2},{4,5},{5,4},{6,7},{7,6},{8,9},{9,8},{10,11... | collective-permute-start | bytes 3145736 | tf_op jit(solution)/shard_map/ppermute | solution.py:235
  62.9 0.7 ladder_own.1.refs_0_
  63.6 0.7 tables.1
  64.3 0.9 collective-permute-done.3.hole
  65.1 0.7 ladder_peer.1
  65.9 17.3 %all_to_all.22.part = bf16[8,512,128]{2,1,0:T(8,128)(2,1)S(1)} all-to-all(bf16[8,512,128]{2,1,0:T(8,128)(2,1)S(1)} %ladder_peer.1), channel_id=1, replica_groups=mesh['x'=4,'zl'=2,'zh'=2,'y'=4,'c'=2] {'x','zl'}, dimensions={0} | all-to-all | bytes 2097152 | tf_op jit(solution)/shard_map/all_to_all | solution.py:245
  83.2 1.3 %spread.1 = bf16[8,16,32,128]{3,2,1,0:T(8,128)(2,1)S(1)} custom-call(bf16[8,16,32,128]{3,2,1,0:T(8,128)(2,1)S(1)} %bitcast.19, bf16[1024,1024]{1,0:T(8,128)(2,1)S(1)} %get-tuple-element.26.perm), custom_call_target="tpu_custom_call" | custom-call | tf_op jit(solution)/shard_map/spread/pallas_call | solution.py:246
  84.5 24.2 %all_to_all.23 = bf16[128,32,128]{2,1,0:T(8,128)(2,1)S(1)} all-to-all(bf16[128,32,128]{2,1,0:T(8,128)(2,1)S(1)} %bitcast.24), channel_id=1, replica_groups=mesh['x'=4,'zl'=2,'zh'=2,'y'=4,'c'=2] {'x','zl','zh','y','c'}, dimensions={0} | all-to-all | bytes 2097152 | tf_op jit(solution)/shard_map/all_to_all | solution.py:253
  108.7 3.9 %final.1 = f32[4096,128]{1,0:T(8,128)} custom-call(bf16[8,512,128]{2,1,0:T(8,128)(2,1)S(1)} %all_to_all.22.part, bf16[8,16,32,128]{3,2,1,0:T(8,128)(2,1)S(1)} %bitcast.22, bf16[1024,1024]{1,0:T(8,128)(2,1)S(1)} %get-tuple-element.27.perm, f32[256,128]{1,0:T(8,128)S(1)} %get-tuple-element.28.virb, f32[16,128]{1,0:T(8,128)S(1)} %get-tuple-element.29.vira, ...), custom_call_target="tpu_custom_call" | custom-call | tf_op jit(solution)/shard_map/final/pallas_call | solution.py:254
  (2 shorter events, 0.0 us)
Async XLA Ops:
  0.0 5.9 %copy-start = (bf16[16,32,1024]{2,1,0:T(8,128)(2,1)S(1)}, bf16[16,32,1024]{2,1,0:T(8,128)(2,1)}, u32[]{:S(2)}) copy-start(bf16[16,32,1024]{2,1,0:T(8,128)(2,1)} %param.5) | copy-start | bytes 3145732
  0.0 5.9 %copy-start.1 = (bf16[16,32,1024]{2,1,0:T(8,128)(2,1)S(1)}, bf16[16,32,1024]{2,1,0:T(8,128)(2,1)}, u32[]{:S(2)}) copy-start(bf16[16,32,1024]{2,1,0:T(8,128)(2,1)} %param.6) | copy-start | bytes 3145732
  0.0 6.7 %collective-permute-start.1 = (bf16[512,1024]{1,0:T(8,128)(2,1)}, bf16[512,1024]{1,0:T(8,128)(2,1)S(1)}, u32[]{:S(2)}, u32[]{:S(2)}) collective-permute-start(bf16[512,1024]{1,0:T(8,128)(2,1)} %bitcast.11), channel_id=1, source_target_pairs={{0,1},{1,0},{2,3},{3,2},{4,5},{5,4},{6,7},{7,6},{8,9},{9,8},{10,11... | collective-permute-start | bytes 3145736 | tf_op jit(solution)/shard_map/ppermute | solution.py:204
  1.4 5.4 %collective-permute-start.2 = (bf16[512,1024]{1,0:T(8,128)(2,1)}, bf16[512,1024]{1,0:T(8,128)(2,1)}, u32[]{:S(2)}, u32[]{:S(2)}) collective-permute-start(bf16[512,1024]{1,0:T(8,128)(2,1)} %bitcast.15), channel_id=1, source_target_pairs={{0,1},{1,0},{2,3},{3,2},{4,5},{5,4},{6,7},{7,6},{8,9},{9,8},{10,11... | collective-permute-start | bytes 3145736 | tf_op jit(solution)/shard_map/ppermute | solution.py:205
  2.2 4.5 %collective-permute-start = (bf16[256,32]{1,0:T(8,128)(2,1)S(1)}, bf16[256,32]{1,0:T(8,128)(2,1)S(1)}, u32[]{:S(2)}, u32[]{:S(2)}) collective-permute-start(bf16[256,32]{1,0:T(8,128)(2,1)S(1)} %reshape.39.fac), channel_id=1, source_target_pairs={{0,1},{1,0},{2,3},{3,2},{4,5},{5,4},{6,7},{7,6},{8,9},{9,8},{10,11... | collective-permute-start | bytes 49160 | tf_op jit(solution)/shard_map/ppermute | solution.py:203
  59.7 5.4 %collective-permute-start.3 = (bf16[512,1024]{1,0:T(8,128)(2,1)S(1)}, bf16[512,1024]{1,0:T(8,128)(2,1)S(1)}, u32[]{:S(2)}, u32[]{:S(2)}) collective-permute-start(bf16[512,1024]{1,0:T(8,128)(2,1)S(1)} %bitcast.20), channel_id=1, source_target_pairs={{0,1},{1,0},{2,3},{3,2},{4,5},{5,4},{6,7},{7,6},{8,9},{9,8},{10,11... | collective-permute-start | bytes 3145736 | tf_op jit(solution)/shard_map/ppermute | solution.py:235

commit v5 on v4

--- a/solution.py
+++ b/solution.py
@@ -93,7 +93,7 @@
         out[rows, :] = total if start is None else total + start[rows, :]
         return carry
 
-    lax.fori_loop(0, 16, one, 0)
+    lax.fori_loop(0, 16, one, 0, unroll=2)
 
 
 def quadratic(core, g, amp, ints):

time: 113 us -> 113 us (level)
  no operation moved by 1% of the time
where the time goes in v5:
time: 113 us
  blocking collectives  91.4 us (81%)
  Pallas kernels  13.7 us (12%)
  starting transfers between devices  5.19 us (5%)
    all_to_all x1, blocking collectives, local(): lax.all_to_all(half_part.reshape(64, 8, 1024), CHIPS, 0, 0, tiled=False)  28.4 us
    all_to_all x1, blocking collectives, local(): lax.all_to_all(outgoing.reshape(128, 32, 128), ALL, 0, 0, tiled=False)  24.3 us
    all_to_all x1, blocking collectives, local(): hole_own = lax.all_to_all(sent, CHIPS, 0, 0, tiled=False).reshape(512, 1024)  21.5 us
    all_to_all x1, blocking collectives, local(): part = lax.all_to_all(chunks, OI, 0, 0, tiled=False)  17.3 us
    pallas_call x1, Pallas kernels, local(): call(final_kernel, 'final', shape((4096, 128), F32), [VMEM] * 6, out_spec...  3.86 us
    ppermute x1, starting transfers between devices, local(): hole_peer = lax.ppermute(hole_own, 'c', SWAP)  3.11 us
    pallas_call x1, Pallas kernels, local(): call(peer_kernel, 'peer', shape((512, 1024)), [SMEM, VMEM, VMEM, VMEM, AN...  3.03 us
  transfers between devices with their start and end apart: 4, of which 1 were waited for; matrix products, arithmetic and copies ran while one was open for 1% of the time, Pallas kernels for 4%

profile of v5, /device:TPU:1, one launch (start us, length us, event | category | flops | bytes accessed | tf_op | source)
XLA Modules:
  0.0 112.9 jit_solution(13882437558807156067)
XLA Ops:
  0.0 0.0 copy-start
  0.0 0.0 copy-start.1
  0.0 1.4 %collective-permute-start.1 = (bf16[512,1024]{1,0:T(8,128)(2,1)}, bf16[512,1024]{1,0:T(8,128)(2,1)S(1)}, u32[]{:S(2)}, u32[]{:S(2)}) collective-permute-start(bf16[512,1024]{1,0:T(8,128)(2,1)} %bitcast.11), channel_id=1, source_target_pairs={{0,1},{1,0},{2,3},{3,2},{4,5},{5,4},{6,7},{7,6},{8,9},{9,8},{10,11... | collective-permute-start | bytes 3145736 | tf_op jit(solution)/shard_map/ppermute | solution.py:204
  1.4 0.0 collective-permute-start.2
  1.4 0.8 reshape.39.fac
  2.2 0.7 collective-permute-start
  2.9 0.8 pad_maximum_fusion
  3.7 0.2 energies.1
  3.9 2.0 %density.1.start = f32[512,1024]{1,0:T(8,128)S(1)} custom-call(s32[1]{0:T(128)} %bitcast.core.half.after, bf16[256,32]{1,0:T(8,128)(2,1)S(1)} %reshape.39.fac), custom_call_target="tpu_custom_call" | custom-call | tf_op jit(solution)/shard_map/density/pallas_call | solution.py:218
  6.0 0.0 copy-done
  6.0 0.0 copy-done.1
  6.0 0.8 own.1.start
  6.8 0.0 collective-permute-done.fac
  6.8 0.0 collective-permute-done.1.amp
  6.8 0.0 collective-permute-done.2.ints
  6.9 3.0 %peer.1 = bf16[512,1024]{1,0:T(8,128)(2,1)S(1)} custom-call(s32[1]{0:T(128)} %bitcast.core.half.after, f32[512,1024]{1,0:T(8,128)S(1)} %own.1.start, bf16[256,32]{1,0:T(8,128)(2,1)S(1)} %collective-permute-done.fac, bf16[512,1024]{1,0:T(8,128)(2,1)S(1)} %collective-permute-done.1.amp, bf16[512,1024]{1,0:T(8,128)(2,1)} %collective-permute-done.2.ints), custom_call_target="tpu_custom_call" | custom-call | tf_op jit(solution)/shard_map/peer/pallas_call | solution.py:220
  9.9 28.4 %all_to_all.20.parts = bf16[64,8,1024]{2,1,0:T(8,128)(2,1)S(1)} all-to-all(bf16[64,8,1024]{2,1,0:T(8,128)(2,1)S(1)} %bitcast.23), channel_id=1, replica_groups=mesh['x'=4,'zl'=2,'zh'=2,'y'=4,'c'=2] {'x','y','zh','zl'}, dimensions={0} | all-to-all | bytes 2097152 | tf_op jit(solution)/shard_map/all_to_all | solution.py:232
  38.3 0.2 sum.1
  38.5 21.5 %all_to_all.21 = bf16[64,8,1024]{2,1,0:T(8,128)(2,1)S(1)} all-to-all(bf16[64,8,1024]{2,1,0:T(8,128)(2,1)S(1)} %sum.1), channel_id=1, replica_groups=mesh['x'=4,'zl'=2,'zh'=2,'y'=4,'c'=2] {'x','y','zh','zl'}, dimensions={0} | all-to-all | bytes 2097152 | tf_op jit(solution)/shard_map/all_to_all | solution.py:234
  60.1 3.1 %collective-permute-start.3 = (bf16[512,1024]{1,0:T(8,128)(2,1)S(1)}, bf16[512,1024]{1,0:T(8,128)(2,1)S(1)}, u32[]{:S(2)}, u32[]{:S(2)}) collective-permute-start(bf16[512,1024]{1,0:T(8,128)(2,1)S(1)} %bitcast.20), channel_id=1, source_target_pairs={{0,1},{1,0},{2,3},{3,2},{4,5},{5,4},{6,7},{7,6},{8,9},{9,8},{10,11... | collective-permute-start | bytes 3145736 | tf_op jit(solution)/shard_map/ppermute | solution.py:235
  63.2 0.7 ladder_own.1.refs_0_
  63.9 0.7 tables.1
  64.6 0.9 collective-permute-done.3.hole
  65.5 0.7 ladder_peer.1
  66.2 17.3 %all_to_all.22.part = bf16[8,512,128]{2,1,0:T(8,128)(2,1)S(1)} all-to-all(bf16[8,512,128]{2,1,0:T(8,128)(2,1)S(1)} %ladder_peer.1), channel_id=1, replica_groups=mesh['x'=4,'zl'=2,'zh'=2,'y'=4,'c'=2] {'x','zl'}, dimensions={0} | all-to-all | bytes 2097152 | tf_op jit(solution)/shard_map/all_to_all | solution.py:245
  83.5 1.3 %spread.1 = bf16[8,16,32,128]{3,2,1,0:T(8,128)(2,1)S(1)} custom-call(bf16[8,16,32,128]{3,2,1,0:T(8,128)(2,1)S(1)} %bitcast.19, bf16[1024,1024]{1,0:T(8,128)(2,1)S(1)} %get-tuple-element.26.perm), custom_call_target="tpu_custom_call" | custom-call | tf_op jit(solution)/shard_map/spread/pallas_call | solution.py:246
  84.8 24.3 %all_to_all.23 = bf16[128,32,128]{2,1,0:T(8,128)(2,1)S(1)} all-to-all(bf16[128,32,128]{2,1,0:T(8,128)(2,1)S(1)} %bitcast.24), channel_id=1, replica_groups=mesh['x'=4,'zl'=2,'zh'=2,'y'=4,'c'=2] {'x','zl','zh','y','c'}, dimensions={0} | all-to-all | bytes 2097152 | tf_op jit(solution)/shard_map/all_to_all | solution.py:253
  109.0 3.9 %final.1 = f32[4096,128]{1,0:T(8,128)} custom-call(bf16[8,512,128]{2,1,0:T(8,128)(2,1)S(1)} %all_to_all.22.part, bf16[8,16,32,128]{3,2,1,0:T(8,128)(2,1)S(1)} %bitcast.22, bf16[1024,1024]{1,0:T(8,128)(2,1)S(1)} %get-tuple-element.27.perm, f32[256,128]{1,0:T(8,128)S(1)} %get-tuple-element.28.virb, f32[16,128]{1,0:T(8,128)S(1)} %get-tuple-element.29.vira, ...), custom_call_target="tpu_custom_call" | custom-call | tf_op jit(solution)/shard_map/final/pallas_call | solution.py:254
  (2 shorter events, 0.0 us)
Async XLA Ops:
  0.0 6.0 %copy-start = (bf16[16,32,1024]{2,1,0:T(8,128)(2,1)S(1)}, bf16[16,32,1024]{2,1,0:T(8,128)(2,1)}, u32[]{:S(2)}) copy-start(bf16[16,32,1024]{2,1,0:T(8,128)(2,1)} %param.5) | copy-start | bytes 3145732
  0.0 6.0 %copy-start.1 = (bf16[16,32,1024]{2,1,0:T(8,128)(2,1)S(1)}, bf16[16,32,1024]{2,1,0:T(8,128)(2,1)}, u32[]{:S(2)}) copy-start(bf16[16,32,1024]{2,1,0:T(8,128)(2,1)} %param.6) | copy-start | bytes 3145732
  0.0 6.8 %collective-permute-start.1 = (bf16[512,1024]{1,0:T(8,128)(2,1)}, bf16[512,1024]{1,0:T(8,128)(2,1)S(1)}, u32[]{:S(2)}, u32[]{:S(2)}) collective-permute-start(bf16[512,1024]{1,0:T(8,128)(2,1)} %bitcast.11), channel_id=1, source_target_pairs={{0,1},{1,0},{2,3},{3,2},{4,5},{5,4},{6,7},{7,6},{8,9},{9,8},{10,11... | collective-permute-start | bytes 3145736 | tf_op jit(solution)/shard_map/ppermute | solution.py:204
  1.4 5.5 %collective-permute-start.2 = (bf16[512,1024]{1,0:T(8,128)(2,1)}, bf16[512,1024]{1,0:T(8,128)(2,1)}, u32[]{:S(2)}, u32[]{:S(2)}) collective-permute-start(bf16[512,1024]{1,0:T(8,128)(2,1)} %bitcast.15), channel_id=1, source_target_pairs={{0,1},{1,0},{2,3},{3,2},{4,5},{5,4},{6,7},{7,6},{8,9},{9,8},{10,11... | collective-permute-start | bytes 3145736 | tf_op jit(solution)/shard_map/ppermute | solution.py:205
  2.2 4.6 %collective-permute-start = (bf16[256,32]{1,0:T(8,128)(2,1)S(1)}, bf16[256,32]{1,0:T(8,128)(2,1)S(1)}, u32[]{:S(2)}, u32[]{:S(2)}) collective-permute-start(bf16[256,32]{1,0:T(8,128)(2,1)S(1)} %reshape.39.fac), channel_id=1, source_target_pairs={{0,1},{1,0},{2,3},{3,2},{4,5},{5,4},{6,7},{7,6},{8,9},{9,8},{10,11... | collective-permute-start | bytes 49160 | tf_op jit(solution)/shard_map/ppermute | solution.py:203
  60.1 5.4 %collective-permute-start.3 = (bf16[512,1024]{1,0:T(8,128)(2,1)S(1)}, bf16[512,1024]{1,0:T(8,128)(2,1)S(1)}, u32[]{:S(2)}, u32[]{:S(2)}) collective-permute-start(bf16[512,1024]{1,0:T(8,128)(2,1)S(1)} %bitcast.20), channel_id=1, source_target_pairs={{0,1},{1,0},{2,3},{3,2},{4,5},{5,4},{6,7},{7,6},{8,9},{9,8},{10,11... | collective-permute-start | bytes 3145736 | tf_op jit(solution)/shard_map/ppermute | solution.py:235
